TPU v7x, 128 devices: a whole 4x4x4 slice. The times are simulated.
128 devices in a mesh: brick: 8 (over y, z_lo), gz: 16 (over x, z_hi, core).
Axes of the slice: x: 4, y: 4, z: 4 (z_hi: 2, z_lo: 2; z = z_hi * 2 + z_lo), core: 2. Of those that a mesh axis runs over, the one named last changes fastest.
Arguments:
- grad_field: float32 [5, 64, 1024, 512], P(None, 'brick', 'gz'), may hold values from -3 to 3
- alpha_coef: float32 [5, 64], P(None, 'brick'), may hold values from 0.3 to 0.4
- metric_inner: float32 [64, 1024], P('brick', 'gz'), may hold values from 0.5 to 2
- metric_outer: float32 [64, 1024], P('brick', 'gz'), may hold values from 0.5 to 2
Outputs:
- adjoint_field: float32 [5, 64, 1024, 512], P(None, 'brick', 'gz')
All inputs are finite; a program needn't handle non-finite values.
Results may differ from a plain program's by a relative error of at most 0.00012.
Values sent between devices are 32-bit elements; how exact they have to be, the bound alone decides.
No kernel may reach another device: no remote copies, remote signals or barrier semaphores. Data moves between devices by JAX's collectives and lax.ppermute only.
A program may use at most 64 MiB of HBM per device.

v0:
```python
import jax
import jax.numpy as jnp
from jax import lax
from jax.experimental import pallas as pl
from jax.experimental.pallas import tpu as pltpu
from jax.sharding import PartitionSpec as P

SMOOTH = 0.2
BF = jnp.bfloat16
F32 = jnp.float32
GRANT = 54
AHEAD = 3
CUT = 2


def iota(shape, axis):
    return lax.broadcasted_iota(jnp.int32, shape, axis)


def alternating(exponent):
    return (1 - 2 * (exponent & 1)).astype(F32)


def split(values):
    high = values.astype(BF)
    low = (values - high.astype(F32)).astype(BF)
    return high, low


def right_side(values):
    high, low = split(values)
    return jnp.concatenate([high, low, high], axis=0)


def left_side(matrix):
    high, low = split(matrix)
    return jnp.concatenate([high, low[:, : matrix.shape[1] // 2]], axis=1)


def dot(left, right):
    return jnp.dot(left, right, preferred_element_type=F32)


def coefs_of(alpha):
    safe = jnp.where(alpha > 0.0, alpha, 0.25)
    ratio = 2.0 * safe / (1.0 + jnp.sqrt(1.0 - 4.0 * safe * safe))
    edge = (4.0 * safe - 1.0) / (12.0 * safe)
    beta = ((safe + 2.0) / 3.0 - edge) / safe
    return jnp.log(ratio), beta, edge


def alpha_column(row):
    n = row.shape[1]
    return jnp.sum(jnp.where(iota((n, n), 0) == iota((n, n), 1), row, 0.0), axis=1, keepdims=True)


def at(coefs, x):
    return tuple(c[x : x + 1] for c in coefs)


def local_parts(cells):
    row = iota((cells, 2 * cells), 0)
    col = iota((cells, 2 * cells), 1) & (cells - 1)
    step = col - row
    size = jnp.abs(step)
    sign = jnp.where(step > 0, 1.0, jnp.where(step < 0, -1.0, 0.0))
    return size.astype(F32), sign * alternating(size), jnp.where(size == 1, sign, 0.0)


def local_matrix(parts, coefs):
    size, sign, near = parts
    log_ratio, beta, edge = coefs
    return beta * (sign * jnp.exp(size * log_ratio)) - edge * near


def state_parts(cells):
    row = iota((16, 2 * cells), 0)
    col = iota((16, 2 * cells), 1) & (cells - 1)
    reach = jnp.where(row == 0, cells - 1 - col, col)
    geometric = jnp.where((row == 0) | (row == 2), alternating(reach), 0.0)
    last = (row == 1) & (col == cells - 1)
    first = (row == 3) & (col == 0)
    return reach.astype(F32), geometric, jnp.where(last | first, 1.0, 0.0)


def state_matrix(parts, coefs, metric):
    reach, geometric, single = parts
    return (geometric * jnp.exp(reach * coefs[0]) + single) * metric


def border_matrix(cells, coefs, after, single):
    row = iota((cells, 128), 0)
    log_ratio, beta, edge = coefs
    reach = jnp.where(after, cells - row, row + 1)
    side = jnp.where(after, 1.0, -1.0)
    geometric = side * alternating(reach) * jnp.exp(reach.astype(F32) * log_ratio)
    beside = jnp.where(reach == 1, -side, 0.0)
    return jnp.where(single, edge * beside, beta * geometric)


def rows_left(matrix):
    high = matrix.astype(BF).astype(F32)
    return jnp.where(iota(matrix.shape, 1) < 64, high, matrix - high).astype(BF)


def pick(values, index_of_lane, alphas):
    lanes = jnp.zeros((1, 128), F32)
    for n in range(values):
        lanes = jnp.where(index_of_lane == n, alphas(n), lanes)
    return lanes


def doubled(row):
    return jnp.concatenate([row, row], axis=1)


def is_odd(axis):
    return lax.rem(lax.axis_index(axis), 2) == 1


def halo_facts(near_ref, far_ref, side, fields, lines, cells):
    x = 0 if side else lines - 1
    near = is_odd("brick") == (side == 0)
    facts = jnp.where(near, near_ref[...], far_ref[...])
    alphas = facts[0:fields, 128:256]
    alpha = jnp.sum(jnp.where(iota(alphas.shape, 1) == x, alphas, 0.0), axis=1, keepdims=True)
    return alpha, doubled(facts[0:1, 0:cells]), doubled(facts[0:1, cells : 2 * cells])


def put_rows(near_ref, far_ref, index, odd, ahead, back):
    near_ref[index] = jnp.where(odd, back, ahead)
    far_ref[index] = jnp.where(odd, ahead, back)


def fetch(field_in, field_scr, sem):
    fields, lines = field_scr.shape[:2]

    def copies(f):
        return [pltpu.make_async_copy(field_in.at[f, x], field_scr.at[f, x], sem.at[f, x]) for x in range(lines)]

    for f in range(AHEAD):
        for copy in copies(f):
            copy.start()

    def ready(f):
        for copy in copies(f):
            copy.wait()

        @pl.when(f + AHEAD < fields)
        def _():
            for copy in copies(f + AHEAD):
                copy.start()

    return ready


def fetch_small(pairs, sem):
    copies = [pltpu.make_async_copy(source, target, sem.at[n]) for n, (source, target) in enumerate(pairs)]
    for copy in copies:
        copy.start()
    return copies


def open_kernel(
    alpha_in, inner_in, outer_in, field_in,
    near_ref, far_ref, edge_near_ref, edge_far_ref, facts_near_ref, facts_far_ref, alpha_ref, inner_ref, outer_ref,
    late_near_ref, late_far_ref, field_ref, sem, field_sem,
):
    fields, lines, cells = field_ref.shape[:3]
    odd_x, odd_z = is_odd("brick"), is_odd("gz")
    small = fetch_small([(alpha_in, alpha_ref), (inner_in, inner_ref), (outer_in, outer_ref)], sem)
    ready = fetch(field_in, field_ref, field_sem)
    for copy in small:
        copy.wait()
    parts = state_parts(cells)

    @pl.loop(0, fields)
    def _(f):
        coefs = coefs_of(alpha_column(alpha_ref[pl.ds(f, 1)]))
        ready(f)
        for x in range(lines):
            matrix = state_matrix(parts, at(coefs, x), doubled(inner_ref[x : x + 1]))
            rows = dot(left_side(matrix), right_side(field_ref[f, x]))
            put_rows(near_ref, far_ref, (f, slice(2 * x, 2 * x + 2)), odd_z, rows[0:2], rows[2:4])

    for f in range(fields):
        near, far, n = (edge_near_ref, edge_far_ref, f) if f < CUT else (late_near_ref, late_far_ref, f - CUT)
        low, high = field_ref[f, 0], field_ref[f, lines - 1]
        near[n] = jnp.where(odd_x, low, high)
        far[n] = jnp.where(odd_x, high, low)
    metrics = jnp.concatenate([inner_ref[...], outer_ref[...]], axis=1)
    for ref, low in ((facts_near_ref, odd_x), (facts_far_ref, jnp.logical_not(odd_x))):
        ref[...] = jnp.zeros_like(ref)
        ref[0:1, 0 : 2 * cells] = jnp.where(low, metrics[0:1], metrics[lines - 1 :])
        ref[0:fields, 128 : 128 + lines] = alpha_ref[...]


def border_term(lines, cells, alphas, f, near_ref, far_ref):
    odd = is_odd("gz")
    near, far = near_ref[f, : 2 * lines], far_ref[f, : 2 * lines]
    states = jnp.concatenate([jnp.where(odd, near, far), jnp.where(odd, far, near)], axis=0)
    k = iota((1, 128), 1) & 31
    line = (k & 15) >> 1
    lane_coefs = coefs_of(pick(lines, line, lambda x: alphas[x : x + 1]))
    matrix = rows_left(border_matrix(cells, lane_coefs, k >= 16, (k & 1) == 1)).astype(F32)
    left = jnp.concatenate([jnp.where(line == x, matrix, 0.0).astype(BF) for x in range(lines)], axis=0)
    high, low = split(states)
    return dot(left, jnp.concatenate([high, low, high, low], axis=0))


def middle_kernel(
    alpha_ref, inner_ref, outer_ref, field_ref, near_ref, far_ref,
    out_ref, near_out_ref, far_out_ref, edge_ref, border_scr, first_scr, local_scr,
):
    fields, lines, cells = field_ref.shape[:3]
    parts = local_parts(cells)
    states = state_parts(cells)
    odd = is_odd("gz")

    @pl.loop(0, fields)
    def _(f):
        alphas = alpha_column(alpha_ref[pl.ds(f, 1)])
        coefs = coefs_of(alphas)
        border_scr[...] = border_term(lines, cells, alphas, f, near_ref, far_ref)
        for x in range(lines):
            matrix = local_matrix(parts, at(coefs, x))
            local_scr[x] = matrix
            left = left_side(matrix * doubled(inner_ref[x : x + 1]))
            first_scr[x] = dot(left, right_side(field_ref[f, x])) + border_scr[cells * x : cells * (x + 1)]
        for x in range(lines):
            middle = (1.0 + 2.0 * SMOOTH) * first_scr[x]
            if x > 0:
                middle = middle - SMOOTH * first_scr[x - 1]
            if x < lines - 1:
                middle = middle - SMOOTH * first_scr[x + 1]
            metric = doubled(outer_ref[x : x + 1])
            left = jnp.concatenate(
                [left_side(local_scr[x] * metric), left_side(state_matrix(states, at(coefs, x), metric))], axis=0
            )
            rows = dot(left, right_side(middle))
            out_ref[f, x] = rows[:cells]
            put_rows(
                near_out_ref, far_out_ref, (f, slice(2 * x, 2 * x + 2)), odd,
                rows[cells : cells + 2], rows[cells + 2 : cells + 4],
            )
        edge_ref[f, 0] = first_scr[0]
        edge_ref[f, 1] = first_scr[lines - 1]


def corner_kernel(near_x_ref, far_x_ref, edge_ref, near_ref, far_ref, near_out_ref, far_out_ref):
    fields, cells, lines = edge_ref.shape[0], edge_ref.shape[2], near_ref.shape[1] // 2
    states = state_parts(cells)
    odd = is_odd("gz")
    for f in range(fields):
        near_out_ref[f, 0 : 2 * lines] = near_ref[f]
        far_out_ref[f, 0 : 2 * lines] = far_ref[f]
    for side in range(2):
        alphas, _, metric = halo_facts(near_x_ref, far_x_ref, side, fields, lines, cells)
        coefs = coefs_of(alphas)
        for f in range(fields):
            matrix = state_matrix(states, at(coefs, f), -SMOOTH * metric)
            rows = dot(left_side(matrix), right_side(edge_ref[f, side]))
            place = 2 * lines + 2 * side
            put_rows(near_out_ref, far_out_ref, (f, slice(place, place + 2)), odd, rows[0:2], rows[2:4])


def prepare_kernel(alpha_ref, outer_ref, near_x_ref, far_x_ref, cells_ref, rows_ref):
    fields, lines = alpha_ref.shape
    cells = outer_ref.shape[1]
    parts = local_parts(cells)
    k = iota((1, 128), 1) & 63
    own = k >= 4 * fields
    field = jnp.where(own, k - 4 * fields, k) >> 2

    @pl.loop(0, fields)
    def _(f):
        coefs = coefs_of(alpha_column(alpha_ref[pl.ds(f, 1)]))
        for side, x in ((0, 0), (1, lines - 1)):
            alphas, metric, _ = halo_facts(near_x_ref, far_x_ref, side, fields, lines, cells)
            own_alphas = jnp.sum(jnp.where(iota((fields, lines), 1) == x, alpha_ref[...], 0.0), axis=1, keepdims=True)
            alpha = jnp.sum(jnp.where(iota((fields, 1), 0) == f, alphas, 0.0), axis=0, keepdims=True)
            outer = left_side(local_matrix(parts, at(coefs, x)) * (-SMOOTH * doubled(outer_ref[x : x + 1])))
            inner = local_matrix(parts, coefs_of(alpha)) * metric
            cells_ref[f, side] = left_side(dot(outer, right_side(inner)))
            halo_lanes = pick(fields, field, lambda n: alphas[n : n + 1])
            own_lanes = pick(fields, field, lambda n: own_alphas[n : n + 1])
            border = border_matrix(cells, coefs_of(jnp.where(own, own_lanes, halo_lanes)), (k & 2) == 2, (k & 1) == 1)
            border = jnp.where(field == f, border, 0.0)
            passed = dot(outer, right_side(jnp.where(own, 0.0, border)))
            rows_ref[f, side] = left_side(passed + jnp.where(own, border, 0.0))


def gather_kernel(near1_ref, far1_ref, near2_ref, far2_ref, near_ref, far_ref):
    fields, lines = near1_ref.shape[0], near1_ref.shape[1] // 2
    odd_z, odd_x = is_odd("gz"), is_odd("brick")
    for half, near, far in ((0, near1_ref, far1_ref), (1, near2_ref, far2_ref)):
        for f in range(fields):
            rows = []
            for side, x in ((0, 0), (1, lines - 1)):
                place = 2 * x if half == 0 else 2 * lines + 2 * side
                one, two = near[f, place : place + 2], far[f, place : place + 2]
                rows.append(jnp.concatenate([jnp.where(odd_z, one, two), jnp.where(odd_z, two, one)], axis=0))
            at_row = 4 * (fields * half + f)
            near_ref[at_row : at_row + 4] = jnp.where(odd_x, rows[0], rows[1])
            far_ref[at_row : at_row + 4] = jnp.where(odd_x, rows[1], rows[0])


def border_kernel(alpha_ref, part_ref, near_ref, far_ref, out_ref, edge_ref, stage, sem):
    fields, lines, cells = part_ref.shape[:3]

    def copies(f):
        return [pltpu.make_async_copy(stage.at[f, x], out_ref.at[f, x], sem.at[f, x]) for x in range(lines)]

    @pl.loop(0, fields)
    def _(f):
        border = border_term(lines, cells, alpha_column(alpha_ref[pl.ds(f, 1)]), f, near_ref, far_ref)
        for x in range(lines):
            value = part_ref[f, x] + border[cells * x : cells * (x + 1)]
            stage[f, x] = value
            if x == 0 or x == lines - 1:
                edge_ref[f, 0 if x == 0 else 1] = value
        for copy in copies(f):
            copy.start()

    @pl.loop(0, fields)
    def _(f):
        for copy in copies(f):
            copy.wait()


def by_side(near_ref, far_ref, index):
    odd = is_odd("brick")
    near, far = near_ref[index], far_ref[index]
    return jnp.where(odd, near, far), jnp.where(odd, far, near)


def late_kernel(
    cells_ref, rows_ref, edge_ref, near1_ref, far1_ref, near2_ref, far2_ref, near_rows_ref, far_rows_ref, _,
    out_ref, state_scr, term_scr, stage, sem,
):
    fields, cells, lines = edge_ref.shape[0], edge_ref.shape[2], out_ref.shape[1]
    copies = []
    for side, rows in enumerate(by_side(near_rows_ref, far_rows_ref, Ellipsis)):
        state_scr[...] = jnp.zeros_like(state_scr)
        state_scr[0 : 8 * fields] = rows
        left = jnp.concatenate([rows_ref[f, side] for f in range(fields)], axis=0)
        term_scr[side] = dot(left, right_side(state_scr[...]))
    for f in range(fields):
        pieces = by_side(near1_ref, far1_ref, f) if f < CUT else by_side(near2_ref, far2_ref, f - CUT)
        for side, halo in enumerate(pieces):
            term = edge_ref[f, side] + term_scr[side, cells * f : cells * (f + 1)]
            stage[f, side] = term + dot(cells_ref[f, side], right_side(halo))
            copies.append(pltpu.make_async_copy(stage.at[f, side], out_ref.at[f, side * (lines - 1)], sem.at[f, side]))
            copies[-1].start()
    for copy in copies:
        copy.wait()


WHOLE = pl.BlockSpec(memory_space=pltpu.VMEM)
ANY = pl.BlockSpec(memory_space=pl.ANY)
HBM = pl.BlockSpec(memory_space=pltpu.HBM)


def call(kernel, limit, ins, out_shape, outs=WHOLE, **options):
    def run(*args):
        return pl.pallas_call(
            kernel,
            in_specs=ins,
            out_specs=outs if isinstance(outs, list) else jax.tree.map(lambda _: outs, out_shape),
            out_shape=out_shape,
            compiler_params=pltpu.CompilerParams(vmem_limit_bytes=limit * 1024 * 1024),
            **options,
        )(*args)

    return run


def swap(axis, near, far):
    count = lax.axis_size(axis)
    ends = count if axis == "gz" else count - 1
    pairs = {"near": [(i, i + 1) for i in range(0, count - 1, 2)], "far": [(i, (i + 1) % count) for i in range(1, ends, 2)]}
    moved = {}
    for kind, value in (("far", far), ("near", near)):
        both = [p for a, b in pairs[kind] for p in ((a, b), (b, a))]
        moved[kind] = lax.ppermute(value, axis, both)
    return moved["near"], moved["far"]


def steps(grad_field, alpha_coef, metric_inner, metric_outer):
    fields, lines, cells, width = grad_field.shape

    def shape(*dims, kind=F32):
        return pltpu.VMEM(dims, kind)

    whole = jax.ShapeDtypeStruct(grad_field.shape, F32)

    rows = shape(fields, 2 * lines, width)
    edge, tail = shape(CUT, cells, width), shape(fields - CUT, cells, width)
    facts, edges = shape(8, 256), shape(fields, 2, cells, width)
    inputs = (alpha_coef, metric_inner, metric_outer, grad_field)
    held = [pltpu.SemaphoreType.DMA((3,)), pltpu.SemaphoreType.DMA((fields, lines))]
    near, far, edge_near, edge_far, facts_near, facts_far, alpha, inner, outer, tail_near, tail_far, field = call(
        open_kernel,
        GRANT,
        [HBM] * 4,
        [rows, rows, edge, edge, facts, facts, *(shape(*a.shape) for a in inputs[:3]), tail, tail, shape(*grad_field.shape)],
        scratch_shapes=held,
    )(*inputs)
    near_one, far_one = swap("gz", near, far)
    near1, far1 = swap("brick", edge_near, edge_far)
    near0, far0 = swap("brick", facts_near, facts_far)

    part, near, far, first = call(
        middle_kernel,
        8,
        [WHOLE] * 6,
        [shape(*grad_field.shape), rows, rows, edges],
        scratch_shapes=[
            pltpu.VMEM((lines * cells, width), F32),
            pltpu.VMEM((lines, cells, width), F32),
            pltpu.VMEM((lines, cells, 2 * cells), F32),
        ],
    )(alpha, inner, outer, field, near_one, far_one)
    rows = shape(fields, 2 * lines + 4, width)
    near, far = call(corner_kernel, 4, [WHOLE] * 5, [rows, rows])(near0, far0, first, near, far)
    near_two, far_two = swap("gz", near, far)
    near2, far2 = swap("brick", tail_near, tail_far)

    matrices = shape(fields, 2, cells, 3 * cells, kind=BF)
    cell_matrix, row_matrix = call(prepare_kernel, 4, [WHOLE] * 4, [matrices, matrices])(alpha, outer, near0, far0)

    rows = shape(8 * fields, width)
    near, far = call(gather_kernel, 2, [WHOLE] * 4, [rows, rows])(near_one, far_one, near_two, far_two)
    near3, far3 = swap("brick", near, far)

    out, edge = call(
        border_kernel,
        16,
        [WHOLE] * 4,
        [whole, edges],
        outs=[HBM, WHOLE],
        scratch_shapes=[pltpu.VMEM(grad_field.shape, F32), pltpu.SemaphoreType.DMA((fields, lines))],
    )(alpha, part, near_two, far_two)

    return call(
        late_kernel,
        8,
        [WHOLE] * 9 + [HBM],
        whole,
        outs=HBM,
        input_output_aliases={9: 0},
        scratch_shapes=[
            pltpu.VMEM((cells, width), F32),
            pltpu.VMEM((2, fields * cells, width), F32),
            pltpu.VMEM((fields, 2, cells, width), F32),
            pltpu.SemaphoreType.DMA((fields, 2)),
        ],
    )(cell_matrix, row_matrix, edge, near1, far1, near2, far2, near3, far3, out)


def solution(mesh):
    placed = (P(None, "brick", "gz", None), P(None, "brick"), P("brick", "gz"), P("brick", "gz"))
    return jax.shard_map(steps, mesh=mesh, in_specs=placed, out_specs=P(None, "brick", "gz", None), check_vma=False)
```

profile of v0, /device:TPU:41, one launch (start us, length us, event | category | flops | bytes accessed | tf_op | source)
XLA Modules:
  0.0 69.4 jit_solution(6787832513511529997)
XLA Ops:
  0.0 4.7 %shard_map.46 = (f32[5,16,512]{2,1,0:T(8,128)S(1)}, f32[5,16,512]{2,1,0:T(8,128)S(1)}, f32[2,64,512]{2,1,0:T(8,128)S(1)}, f32[2,64,512]{2,1,0:T(8,128)S(1)}, f32...) custom-call(f32[5,8]{1,0:T(8,128)} %alpha_in.1, ...), custom_call_target="tpu_custom_call" | custom-call | tf_op jit(solution)/shard_map/pallas_call | solution.py:366
  4.7 0.8 %collective-permute-start.2 = (f32[5,16,512]{2,1,0:T(8,128)S(1)}, f32[5,16,512]{2,1,0:T(8,128)S(1)}, u32[]{:S(2)}, u32[]{:S(2)}) collective-permute-start(f32[5,16,512]{2,1,0:T(8,128)S(1)} %get-tuple-element.37), channel_id=1, source_target_pairs={{0,1},{1,0},{2,3},{3,2},{4,5},{5,4},{6,7},{7,6},{8,9},{9,8},{10,11... | collective-permute-start | bytes 491528 | tf_op jit(solution)/shard_map/ppermute | solution.py:385
  5.5 2.7 %collective-permute-start.3 = (f32[5,16,512]{2,1,0:T(8,128)S(1)}, f32[5,16,512]{2,1,0:T(8,128)S(1)}, u32[]{:S(2)}, u32[]{:S(2)}) collective-permute-start(f32[5,16,512]{2,1,0:T(8,128)S(1)} %get-tuple-element.38), channel_id=1, source_target_pairs={{1,2},{2,1},{3,4},{4,3},{5,6},{6,5},{7,8},{8,7},{9,10},{10,9},{11,... | collective-permute-start | bytes 491528 | tf_op jit(solution)/shard_map/ppermute | solution.py:385
  8.1 0.7 %collective-permute-start = (f32[8,256]{1,0:T(8,128)S(1)}, f32[8,256]{1,0:T(8,128)S(1)}, u32[]{:S(2)}, u32[]{:S(2)}) collective-permute-start(f32[8,256]{1,0:T(8,128)S(1)} %get-tuple-element.31), channel_id=1, source_target_pairs={{0,16},{16,0},{32,48},{48,32},{64,80},{80,64},{96,112},{112,96},{1... | collective-permute-start | bytes 24584 | tf_op jit(solution)/shard_map/ppermute | solution.py:385
  8.9 3.6 %collective-permute-start.1 = (f32[8,256]{1,0:T(8,128)S(1)}, f32[8,256]{1,0:T(8,128)S(1)}, u32[]{:S(2)}, u32[]{:S(2)}) collective-permute-start(f32[8,256]{1,0:T(8,128)S(1)} %get-tuple-element.32), channel_id=1, source_target_pairs={{16,32},{32,16},{48,64},{64,48},{80,96},{96,80},{17,33},{33,17},{4... | collective-permute-start | bytes 24584 | tf_op jit(solution)/shard_map/ppermute | solution.py:385
  12.5 0.0 collective-permute-done.2.near_ref.near1_ref
  12.5 1.0 %collective-permute-done.3.far_ref.far1_ref = f32[5,16,512]{2,1,0:T(8,128)S(1)} collective-permute-done((f32[5,16,512]{2,1,0:T(8,128)S(1)}, f32[5,16,512]{2,1,0:T(8,128)S(1)}, u32[]{:S(2)}, u32[]{:S(2)}) %collective-permute-start.3) | collective-permute-done | bytes 163872 | tf_op jit(solution)/shard_map/ppermute | solution.py:385
  13.6 5.6 %shard_map.48 = (f32[5,8,64,512]{3,2,1,0:T(8,128)S(1)}, f32[5,16,512]{2,1,0:T(8,128)S(1)}, f32[5,16,512]{2,1,0:T(8,128)S(1)}, f32[5,2,64,512]{3,2,1,0:T(8,128)S(1)}) custom-call(f32[5,8]{1,0:T(8,128)S(1)} %get-tuple-element.29.alpha_ref, f32[8,64]{1,0:T(8,128)S(1)} %get-tuple-element.35.inner_ref, f32[8,64]{1,0:T(8,128)S(1)} %get-tuple-element.30.outer_ref, ...), custom_call_target="tpu_custom_call" | custom-call | tf_op jit(solution)/shard_map/pallas_call | solution.py:366
  19.1 0.0 collective-permute-done.near_x_ref
  19.1 0.0 collective-permute-done.1.far_x_ref
  19.1 0.5 shard_map.49
  19.6 2.2 %collective-permute-start.4 = (f32[5,20,512]{2,1,0:T(8,128)S(1)}, f32[5,20,512]{2,1,0:T(8,128)S(1)}, u32[]{:S(2)}, u32[]{:S(2)}) collective-permute-start(f32[5,20,512]{2,1,0:T(8,128)S(1)} %get-tuple-element.43), channel_id=1, source_target_pairs={{0,1},{1,0},{2,3},{3,2},{4,5},{5,4},{6,7},{7,6},{8,9},{9,8},{10,11... | collective-permute-start | bytes 614408 | tf_op jit(solution)/shard_map/ppermute | solution.py:385
  21.9 0.0 collective-permute-start.8
  21.9 4.1 %collective-permute-start.9 = (f32[3,64,512]{2,1,0:T(8,128)S(1)}, f32[3,64,512]{2,1,0:T(8,128)S(1)}, u32[]{:S(2)}, u32[]{:S(2)}) collective-permute-start(f32[3,64,512]{2,1,0:T(8,128)S(1)} %get-tuple-element.49), channel_id=1, source_target_pairs={{16,32},{32,16},{48,64},{64,48},{80,96},{96,80},{17,33},{33,17},{4... | collective-permute-start | bytes 1179656 | tf_op jit(solution)/shard_map/ppermute | solution.py:385
  26.0 0.1 collective-permute-start.6
  26.1 1.5 %collective-permute-start.5 = (f32[5,20,512]{2,1,0:T(8,128)S(1)}, f32[5,20,512]{2,1,0:T(8,128)S(1)}, u32[]{:S(2)}, u32[]{:S(2)}) collective-permute-start(f32[5,20,512]{2,1,0:T(8,128)S(1)} %get-tuple-element.44), channel_id=1, source_target_pairs={{1,2},{2,1},{3,4},{4,3},{5,6},{6,5},{7,8},{8,7},{9,10},{10,9},{11,... | collective-permute-start | bytes 614408 | tf_op jit(solution)/shard_map/ppermute | solution.py:385
  27.5 0.0 collective-permute-done.4.near_ref.near2_ref
  27.5 4.9 %collective-permute-start.7 = (f32[2,64,512]{2,1,0:T(8,128)S(1)}, f32[2,64,512]{2,1,0:T(8,128)S(1)}, u32[]{:S(2)}, u32[]{:S(2)}) collective-permute-start(f32[2,64,512]{2,1,0:T(8,128)S(1)} %get-tuple-element.47), channel_id=1, source_target_pairs={{16,32},{32,16},{48,64},{64,48},{80,96},{96,80},{17,33},{33,17},{4... | collective-permute-start | bytes 786440 | tf_op jit(solution)/shard_map/ppermute | solution.py:385
  32.4 25.3 %collective-permute-done.5.far_ref.far2_ref = f32[5,20,512]{2,1,0:T(8,128)S(1)} collective-permute-done((f32[5,20,512]{2,1,0:T(8,128)S(1)}, f32[5,20,512]{2,1,0:T(8,128)S(1)}, u32[]{:S(2)}, u32[]{:S(2)}) %collective-permute-start.5) | collective-permute-done | bytes 204832 | tf_op jit(solution)/shard_map/ppermute | solution.py:385
  57.7 0.1 shard_map.51
  57.8 2.0 %collective-permute-start.10 = (f32[40,512]{1,0:T(8,128)S(1)}, f32[40,512]{1,0:T(8,128)S(1)}, u32[]{:S(2)}, u32[]{:S(2)}) collective-permute-start(f32[40,512]{1,0:T(8,128)S(1)} %get-tuple-element.50), channel_id=1, source_target_pairs={{0,16},{16,0},{32,48},{48,32},{64,80},{80,64},{96,112},{112,96},{1... | collective-permute-start | bytes 245768 | tf_op jit(solution)/shard_map/ppermute | solution.py:385
  59.8 0.0 collective-permute-done.6.near1_ref
  59.8 2.9 %collective-permute-start.11 = (f32[40,512]{1,0:T(8,128)S(1)}, f32[40,512]{1,0:T(8,128)S(1)}, u32[]{:S(2)}, u32[]{:S(2)}) collective-permute-start(f32[40,512]{1,0:T(8,128)S(1)} %get-tuple-element.51), channel_id=1, source_target_pairs={{16,32},{32,16},{48,64},{64,48},{80,96},{96,80},{17,33},{33,17},{4... | collective-permute-start | bytes 245768 | tf_op jit(solution)/shard_map/ppermute | solution.py:385
  62.8 1.7 %shard_map.47 = (bf16[5,2,64,192]{3,2,1,0:T(8,128)(2,1)S(1)}, bf16[5,2,64,192]{3,2,1,0:T(8,128)(2,1)S(1)}) custom-call(f32[5,8]{1,0:T(8,128)S(1)} %get-tuple-element.29.alpha_ref, f32[8,64]{1,0:T(8,128)S(1)} %get-tuple-element.30.outer_ref, f32[8,256]{1,0:T(8,128)S(1)} %collective-permute-done.near_x_ref, f32[8,256]{1,0:T(8,128)S(1)} %collective-permute-done.1.far_x_ref), custom_call_target="tpu_custom_call" | custom-call | tf_op jit(solution)/shard_map/pallas_call | solution.py:366
  64.5 3.3 %shard_map.50 = (f32[5,8,64,512]{3,2,1,0:T(8,128)}, f32[5,2,64,512]{3,2,1,0:T(8,128)S(1)}) custom-call(f32[5,8]{1,0:T(8,128)S(1)} %get-tuple-element.29.alpha_ref, f32[5,8,64,512]{3,2,1,0:T(8,128)S(1)} %get-tuple-element.39.part_ref, f32[5,20,512]{2,1,0:T(8,128)S(1)} %collective-permute-done.4.near_ref.near2_ref, ...), custom_call_target="tpu_custom_call" | custom-call | tf_op jit(solution)/shard_map/pallas_call | solution.py:366
  67.8 0.0 collective-permute-done.7.far1_ref
  67.8 0.0 collective-permute-done.8.near2_ref
  67.8 0.0 collective-permute-done.9.far2_ref
  67.8 0.0 collective-permute-done.10.near_rows_ref
  67.9 0.0 collective-permute-done.11.far_rows_ref
  67.9 1.5 %shard_map.52 = f32[5,8,64,512]{3,2,1,0:T(8,128)} custom-call(bf16[5,2,64,192]{3,2,1,0:T(8,128)(2,1)S(1)} %get-tuple-element.33.cells_ref, bf16[5,2,64,192]{3,2,1,0:T(8,128)(2,1)S(1)} %get-tuple-element.34.rows_ref, f32[5,2,64,512]{3,2,1,0:T(8,128)S(1)} %get-tuple-element.45.edge_ref, ...), custom_call_target="tpu_custom_call", output_to_operand_aliasing={{}: (9, {})} | custom-call | tf_op jit(solution)/shard_map/pallas_call | solution.py:366
Async XLA Ops:
  4.7 7.8 %collective-permute-start.2 = (f32[5,16,512]{2,1,0:T(8,128)S(1)}, f32[5,16,512]{2,1,0:T(8,128)S(1)}, u32[]{:S(2)}, u32[]{:S(2)}) collective-permute-start(f32[5,16,512]{2,1,0:T(8,128)S(1)} %get-tuple-element.37), channel_id=1, source_target_pairs={{0,1},{1,0},{2,3},{3,2},{4,5},{5,4},{6,7},{7,6},{8,9},{9,8},{10,11... | collective-permute-start | bytes 491528 | tf_op jit(solution)/shard_map/ppermute | solution.py:385
  5.5 8.1 %collective-permute-start.3 = (f32[5,16,512]{2,1,0:T(8,128)S(1)}, f32[5,16,512]{2,1,0:T(8,128)S(1)}, u32[]{:S(2)}, u32[]{:S(2)}) collective-permute-start(f32[5,16,512]{2,1,0:T(8,128)S(1)} %get-tuple-element.38), channel_id=1, source_target_pairs={{1,2},{2,1},{3,4},{4,3},{5,6},{6,5},{7,8},{8,7},{9,10},{10,9},{11,... | collective-permute-start | bytes 491528 | tf_op jit(solution)/shard_map/ppermute | solution.py:385
  8.1 11.0 %collective-permute-start = (f32[8,256]{1,0:T(8,128)S(1)}, f32[8,256]{1,0:T(8,128)S(1)}, u32[]{:S(2)}, u32[]{:S(2)}) collective-permute-start(f32[8,256]{1,0:T(8,128)S(1)} %get-tuple-element.31), channel_id=1, source_target_pairs={{0,16},{16,0},{32,48},{48,32},{64,80},{80,64},{96,112},{112,96},{1... | collective-permute-start | bytes 24584 | tf_op jit(solution)/shard_map/ppermute | solution.py:385
  8.9 10.3 %collective-permute-start.1 = (f32[8,256]{1,0:T(8,128)S(1)}, f32[8,256]{1,0:T(8,128)S(1)}, u32[]{:S(2)}, u32[]{:S(2)}) collective-permute-start(f32[8,256]{1,0:T(8,128)S(1)} %get-tuple-element.32), channel_id=1, source_target_pairs={{16,32},{32,16},{48,64},{64,48},{80,96},{96,80},{17,33},{33,17},{4... | collective-permute-start | bytes 24584 | tf_op jit(solution)/shard_map/ppermute | solution.py:385
  19.6 7.9 %collective-permute-start.4 = (f32[5,20,512]{2,1,0:T(8,128)S(1)}, f32[5,20,512]{2,1,0:T(8,128)S(1)}, u32[]{:S(2)}, u32[]{:S(2)}) collective-permute-start(f32[5,20,512]{2,1,0:T(8,128)S(1)} %get-tuple-element.43), channel_id=1, source_target_pairs={{0,1},{1,0},{2,3},{3,2},{4,5},{5,4},{6,7},{7,6},{8,9},{9,8},{10,11... | collective-permute-start | bytes 614408 | tf_op jit(solution)/shard_map/ppermute | solution.py:385
  21.9 45.9 %collective-permute-start.8 = (f32[3,64,512]{2,1,0:T(8,128)S(1)}, f32[3,64,512]{2,1,0:T(8,128)S(1)}, u32[]{:S(2)}, u32[]{:S(2)}) collective-permute-start(f32[3,64,512]{2,1,0:T(8,128)S(1)} %get-tuple-element.48), channel_id=1, source_target_pairs={{0,16},{16,0},{32,48},{48,32},{64,80},{80,64},{96,112},{112,96},{1... | collective-permute-start | bytes 1179656 | tf_op jit(solution)/shard_map/ppermute | solution.py:385
  21.9 45.9 %collective-permute-start.9 = (f32[3,64,512]{2,1,0:T(8,128)S(1)}, f32[3,64,512]{2,1,0:T(8,128)S(1)}, u32[]{:S(2)}, u32[]{:S(2)}) collective-permute-start(f32[3,64,512]{2,1,0:T(8,128)S(1)} %get-tuple-element.49), channel_id=1, source_target_pairs={{16,32},{32,16},{48,64},{64,48},{80,96},{96,80},{17,33},{33,17},{4... | collective-permute-start | bytes 1179656 | tf_op jit(solution)/shard_map/ppermute | solution.py:385
  26.0 33.9 %collective-permute-start.6 = (f32[2,64,512]{2,1,0:T(8,128)S(1)}, f32[2,64,512]{2,1,0:T(8,128)S(1)}, u32[]{:S(2)}, u32[]{:S(2)}) collective-permute-start(f32[2,64,512]{2,1,0:T(8,128)S(1)} %get-tuple-element.46), channel_id=1, source_target_pairs={{0,16},{16,0},{32,48},{48,32},{64,80},{80,64},{96,112},{112,96},{1... | collective-permute-start | bytes 786440 | tf_op jit(solution)/shard_map/ppermute | solution.py:385
  26.1 31.6 %collective-permute-start.5 = (f32[5,20,512]{2,1,0:T(8,128)S(1)}, f32[5,20,512]{2,1,0:T(8,128)S(1)}, u32[]{:S(2)}, u32[]{:S(2)}) collective-permute-start(f32[5,20,512]{2,1,0:T(8,128)S(1)} %get-tuple-element.44), channel_id=1, source_target_pairs={{1,2},{2,1},{3,4},{4,3},{5,6},{6,5},{7,8},{8,7},{9,10},{10,9},{11,... | collective-permute-start | bytes 614408 | tf_op jit(solution)/shard_map/ppermute | solution.py:385
  27.5 40.3 %collective-permute-start.7 = (f32[2,64,512]{2,1,0:T(8,128)S(1)}, f32[2,64,512]{2,1,0:T(8,128)S(1)}, u32[]{:S(2)}, u32[]{:S(2)}) collective-permute-start(f32[2,64,512]{2,1,0:T(8,128)S(1)} %get-tuple-element.47), channel_id=1, source_target_pairs={{16,32},{32,16},{48,64},{64,48},{80,96},{96,80},{17,33},{33,17},{4... | collective-permute-start | bytes 786440 | tf_op jit(solution)/shard_map/ppermute | solution.py:385
  57.8 10.1 %collective-permute-start.10 = (f32[40,512]{1,0:T(8,128)S(1)}, f32[40,512]{1,0:T(8,128)S(1)}, u32[]{:S(2)}, u32[]{:S(2)}) collective-permute-start(f32[40,512]{1,0:T(8,128)S(1)} %get-tuple-element.50), channel_id=1, source_target_pairs={{0,16},{16,0},{32,48},{48,32},{64,80},{80,64},{96,112},{112,96},{1... | collective-permute-start | bytes 245768 | tf_op jit(solution)/shard_map/ppermute | solution.py:385
  59.8 8.0 %collective-permute-start.11 = (f32[40,512]{1,0:T(8,128)S(1)}, f32[40,512]{1,0:T(8,128)S(1)}, u32[]{:S(2)}, u32[]{:S(2)}) collective-permute-start(f32[40,512]{1,0:T(8,128)S(1)} %get-tuple-element.51), channel_id=1, source_target_pairs={{16,32},{32,16},{48,64},{64,48},{80,96},{96,80},{17,33},{33,17},{4... | collective-permute-start | bytes 245768 | tf_op jit(solution)/shard_map/ppermute | solution.py:385
where the time goes:
time: 70.8 us; the launch traced here: 69.4 us
  waiting for transfers between devices  26.4 us (37%)
  starting transfers between devices  25.5 us (36%)
  Pallas kernels  17.4 us (25%)
    ppermute x12, waiting for transfers between devices, swap(): moved[kind] = lax.ppermute(value, axis, both)  26.4 us
    ppermute x12, starting transfers between devices, swap(): moved[kind] = lax.ppermute(value, axis, both)  25.5 us
    pallas_call x7, Pallas kernels, run(): pl.pallas_call(kernel, in_specs=ins, out_specs=outs if isinstance(outs, l...  17.4 us
  transfers between devices with their start and end apart: 12, of which 2 were waited for; matrix products, arithmetic and copies ran while one was open for 0% of the time, Pallas kernels for 15%

commit v1 on v0

--- a/solution.py
+++ b/solution.py
@@ -10,7 +10,6 @@
 F32 = jnp.float32
 GRANT = 54
 AHEAD = 3
-CUT = 2
 
 
 def iota(shape, axis):
@@ -121,15 +120,10 @@
 def halo_facts(near_ref, far_ref, side, fields, lines, cells):
     x = 0 if side else lines - 1
     near = is_odd("brick") == (side == 0)
-    facts = jnp.where(near, near_ref[...], far_ref[...])
+    facts = jnp.where(near, near_ref[cells : cells + 8, 0:256], far_ref[cells : cells + 8, 0:256])
     alphas = facts[0:fields, 128:256]
     alpha = jnp.sum(jnp.where(iota(alphas.shape, 1) == x, alphas, 0.0), axis=1, keepdims=True)
     return alpha, doubled(facts[0:1, 0:cells]), doubled(facts[0:1, cells : 2 * cells])
-
-
-def put_rows(near_ref, far_ref, index, odd, ahead, back):
-    near_ref[index] = jnp.where(odd, back, ahead)
-    far_ref[index] = jnp.where(odd, ahead, back)
 
 
 def fetch(field_in, field_scr, sem):
@@ -161,107 +155,173 @@
     return copies
 
 
+def pack_kernel(
+    alpha_in, inner_in, outer_in, field_in, near_ref, far_ref, alpha_ref, inner_ref, outer_ref, sem
+):
+    fields, lines = alpha_ref.shape
+    cells = inner_ref.shape[1]
+    odd = is_odd("brick")
+    near_x = jnp.where(odd, 0, lines - 1)
+    copies = fetch_small(
+        [
+            (alpha_in, alpha_ref),
+            (inner_in, inner_ref),
+            (outer_in, outer_ref),
+            (field_in.at[0, near_x], near_ref.at[pl.ds(0, cells)]),
+            (field_in.at[0, lines - 1 - near_x], far_ref.at[pl.ds(0, cells)]),
+        ],
+        sem,
+    )
+    for copy in copies:
+        copy.wait()
+    metrics = jnp.concatenate([inner_ref[...], outer_ref[...]], axis=1)
+    for ref, low in ((near_ref, odd), (far_ref, jnp.logical_not(odd))):
+        ref[cells:] = jnp.zeros_like(ref[cells:])
+        ref[cells : cells + 1, 0 : 2 * cells] = jnp.where(low, metrics[0:1], metrics[lines - 1 :])
+        ref[cells : cells + fields, 128 : 128 + lines] = alpha_ref[...]
+
+
 def open_kernel(
-    alpha_in, inner_in, outer_in, field_in,
-    near_ref, far_ref, edge_near_ref, edge_far_ref, facts_near_ref, facts_far_ref, alpha_ref, inner_ref, outer_ref,
-    late_near_ref, late_far_ref, field_ref, sem, field_sem,
+    alpha_ref, inner_ref, outer_ref, field_in,
+    part_ref, own_ref, next_ref, edge_ref, line_near_ref, line_far_ref, field_ref, first_scr, local_scr, field_sem,
 ):
     fields, lines, cells = field_ref.shape[:3]
-    odd_x, odd_z = is_odd("brick"), is_odd("gz")
-    small = fetch_small([(alpha_in, alpha_ref), (inner_in, inner_ref), (outer_in, outer_ref)], sem)
+    odd = is_odd("brick")
     ready = fetch(field_in, field_ref, field_sem)
-    for copy in small:
-        copy.wait()
-    parts = state_parts(cells)
+    parts = local_parts(cells)
+    states = state_parts(cells)
+
+    def put(ref, f, x, rows):
+        ref[f, 2 * x : 2 * x + 2] = rows[0:2]
+        ref[f, 2 * (lines + x) : 2 * (lines + x) + 2] = rows[2:4]
 
     @pl.loop(0, fields)
     def _(f):
         coefs = coefs_of(alpha_column(alpha_ref[pl.ds(f, 1)]))
         ready(f)
+
+        def left(x, metric):
+            local = left_side(local_scr[x] * metric)
+            return jnp.concatenate([local, left_side(state_matrix(states, at(coefs, x), metric))], axis=0)
+
         for x in range(lines):
-            matrix = state_matrix(parts, at(coefs, x), doubled(inner_ref[x : x + 1]))
-            rows = dot(left_side(matrix), right_side(field_ref[f, x]))
-            put_rows(near_ref, far_ref, (f, slice(2 * x, 2 * x + 2)), odd_z, rows[0:2], rows[2:4])
-
-    for f in range(fields):
-        near, far, n = (edge_near_ref, edge_far_ref, f) if f < CUT else (late_near_ref, late_far_ref, f - CUT)
-        low, high = field_ref[f, 0], field_ref[f, lines - 1]
-        near[n] = jnp.where(odd_x, low, high)
-        far[n] = jnp.where(odd_x, high, low)
-    metrics = jnp.concatenate([inner_ref[...], outer_ref[...]], axis=1)
-    for ref, low in ((facts_near_ref, odd_x), (facts_far_ref, jnp.logical_not(odd_x))):
-        ref[...] = jnp.zeros_like(ref)
-        ref[0:1, 0 : 2 * cells] = jnp.where(low, metrics[0:1], metrics[lines - 1 :])
-        ref[0:fields, 128 : 128 + lines] = alpha_ref[...]
-
-
-def border_term(lines, cells, alphas, f, near_ref, far_ref):
-    odd = is_odd("gz")
-    near, far = near_ref[f, : 2 * lines], far_ref[f, : 2 * lines]
-    states = jnp.concatenate([jnp.where(odd, near, far), jnp.where(odd, far, near)], axis=0)
-    k = iota((1, 128), 1) & 31
-    line = (k & 15) >> 1
-    lane_coefs = coefs_of(pick(lines, line, lambda x: alphas[x : x + 1]))
-    matrix = rows_left(border_matrix(cells, lane_coefs, k >= 16, (k & 1) == 1)).astype(F32)
-    left = jnp.concatenate([jnp.where(line == x, matrix, 0.0).astype(BF) for x in range(lines)], axis=0)
-    high, low = split(states)
-    return dot(left, jnp.concatenate([high, low, high, low], axis=0))
-
-
-def middle_kernel(
-    alpha_ref, inner_ref, outer_ref, field_ref, near_ref, far_ref,
-    out_ref, near_out_ref, far_out_ref, edge_ref, border_scr, first_scr, local_scr,
-):
-    fields, lines, cells = field_ref.shape[:3]
-    parts = local_parts(cells)
-    states = state_parts(cells)
-    odd = is_odd("gz")
-
-    @pl.loop(0, fields)
-    def _(f):
-        alphas = alpha_column(alpha_ref[pl.ds(f, 1)])
-        coefs = coefs_of(alphas)
-        border_scr[...] = border_term(lines, cells, alphas, f, near_ref, far_ref)
-        for x in range(lines):
-            matrix = local_matrix(parts, at(coefs, x))
-            local_scr[x] = matrix
-            left = left_side(matrix * doubled(inner_ref[x : x + 1]))
-            first_scr[x] = dot(left, right_side(field_ref[f, x])) + border_scr[cells * x : cells * (x + 1)]
+            local_scr[x] = local_matrix(parts, at(coefs, x))
+            rows = dot(left(x, doubled(inner_ref[x : x + 1])), right_side(field_ref[f, x]))
+            first_scr[x] = rows[:cells]
+            put(own_ref, f, x, rows[cells:])
         for x in range(lines):
             middle = (1.0 + 2.0 * SMOOTH) * first_scr[x]
             if x > 0:
                 middle = middle - SMOOTH * first_scr[x - 1]
             if x < lines - 1:
                 middle = middle - SMOOTH * first_scr[x + 1]
-            metric = doubled(outer_ref[x : x + 1])
-            left = jnp.concatenate(
-                [left_side(local_scr[x] * metric), left_side(state_matrix(states, at(coefs, x), metric))], axis=0
-            )
-            rows = dot(left, right_side(middle))
-            out_ref[f, x] = rows[:cells]
-            put_rows(
-                near_out_ref, far_out_ref, (f, slice(2 * x, 2 * x + 2)), odd,
-                rows[cells : cells + 2], rows[cells + 2 : cells + 4],
-            )
+            rows = dot(left(x, doubled(outer_ref[x : x + 1])), right_side(middle))
+            part_ref[f, x] = rows[:cells]
+            put(next_ref, f, x, rows[cells:])
         edge_ref[f, 0] = first_scr[0]
         edge_ref[f, 1] = first_scr[lines - 1]
 
-
-def corner_kernel(near_x_ref, far_x_ref, edge_ref, near_ref, far_ref, near_out_ref, far_out_ref):
-    fields, cells, lines = edge_ref.shape[0], edge_ref.shape[2], near_ref.shape[1] // 2
+    for f in range(1, fields):
+        low, high = field_ref[f, 0], field_ref[f, lines - 1]
+        line_near_ref[f - 1] = jnp.where(odd, low, high)
+        line_far_ref[f - 1] = jnp.where(odd, high, low)
+
+
+def corner_kernel(
+    near_x_ref, far_x_ref, outer_ref, edge_ref, own_ref, next_ref, near_ref, far_ref, ahead_ref, back_ref
+):
+    fields, cells, lines = edge_ref.shape[0], edge_ref.shape[2], own_ref.shape[1] // 4
+    half = 2 * lines
     states = state_parts(cells)
     odd = is_odd("gz")
     for f in range(fields):
-        near_out_ref[f, 0 : 2 * lines] = near_ref[f]
-        far_out_ref[f, 0 : 2 * lines] = far_ref[f]
+        for ref, start in ((ahead_ref, 0), (back_ref, half)):
+            ref[f, 0:half] = own_ref[f, start : start + half]
+            ref[f, half : 2 * half] = next_ref[f, start : start + half]
+            ref[f, 2 * half + 4 :] = jnp.zeros_like(ref[f, 2 * half + 4 :])
+            if 2 * f < lines:
+                ref[f, 2 * half + 4 :, 0:cells] = outer_ref[2 * f : 2 * f + 2]
     for side in range(2):
         alphas, _, metric = halo_facts(near_x_ref, far_x_ref, side, fields, lines, cells)
         coefs = coefs_of(alphas)
+        place = 2 * half + 2 * side
         for f in range(fields):
             matrix = state_matrix(states, at(coefs, f), -SMOOTH * metric)
             rows = dot(left_side(matrix), right_side(edge_ref[f, side]))
-            place = 2 * lines + 2 * side
-            put_rows(near_out_ref, far_out_ref, (f, slice(place, place + 2)), odd, rows[0:2], rows[2:4])
+            ahead_ref[f, place : place + 2] = rows[0:2]
+            back_ref[f, place : place + 2] = rows[2:4]
+        for ref in (ahead_ref, back_ref):
+            ref[fields - 1, 2 * half + 4 + side : 2 * half + 5 + side, 0:cells] = metric[:, 0:cells]
+    near_ref[...] = jnp.where(odd, back_ref[...], ahead_ref[...])
+    far_ref[...] = jnp.where(odd, ahead_ref[...], back_ref[...])
+
+
+def border_lanes(lines, cells, alphas):
+    k = iota((1, 128), 1) & 31
+    line = (k & 15) >> 1
+    lane_coefs = coefs_of(pick(lines, line, lambda x: alphas[x : x + 1]))
+    return border_matrix(cells, lane_coefs, k >= 16, (k & 1) == 1), line, k >= 16
+
+
+def spread(line, x):
+    beside = (line == x - 1) | (line == x + 1)
+    return jnp.where(line == x, 1.0 + 2.0 * SMOOTH, jnp.where(beside, -SMOOTH, 0.0))
+
+
+def four_pieces(states):
+    high, low = split(states)
+    return jnp.concatenate([high, low, high, low], axis=0)
+
+
+def join_kernel(
+    alpha_ref, near_x_ref, far_x_ref, own_ref, near_ref, far_ref,
+    first_ref, second_ref, near_out_ref, far_out_ref, behind_scr, beyond_scr,
+):
+    fields, lines = alpha_ref.shape
+    half, cells = 2 * lines, near_x_ref.shape[0] - 8
+    states = state_parts(cells)
+    odd_z, odd_x = is_odd("gz"), is_odd("brick")
+    behind_scr[...] = jnp.where(odd_z, near_ref[...], far_ref[...])
+    beyond_scr[...] = jnp.where(odd_z, far_ref[...], near_ref[...])
+    halo = [halo_facts(near_x_ref, far_x_ref, side, fields, lines, cells)[0] for side in range(2)]
+
+    def metric_of(ref, line):
+        f, row = (line // 2, line % 2) if line < lines else (fields - 1, line - lines)
+        return doubled(ref[f, 2 * half + 4 + row : 2 * half + 5 + row, 0:cells])
+
+    for f in range(fields):
+        alphas = alpha_column(alpha_ref[f : f + 1])
+        coefs = coefs_of(alphas)
+        border, line, after = border_lanes(lines, cells, alphas)
+
+        def caused(coef, place, weight):
+            left = jnp.concatenate(
+                [left_side(state_matrix(states, coef, metric_of(ref, place))) for ref in (behind_scr, beyond_scr)], axis=0
+            )
+            rows = dot(left, right_side(border * weight))
+            return jnp.where(after, rows[0:2], 0.0), jnp.where(after, 0.0, rows[18:20])
+
+        pairs = [caused(at(coefs, x), x, spread(line, x)) for x in range(lines)]
+        for side, x in ((0, 0), (1, lines - 1)):
+            coef = coefs_of(halo[side][f : f + 1])
+            pairs.append(caused(coef, lines + side, jnp.where(line == x, -SMOOTH, 0.0)))
+        pad = [jnp.zeros((4, 128), F32)]
+        left = jnp.concatenate([p[0] for p in pairs] + pad + [p[1] for p in pairs] + pad, axis=0)
+        added = dot(rows_left(left), four_pieces(own_ref[f]))
+        rows = []
+        for n, ref in enumerate((behind_scr, beyond_scr)):
+            extra = added[24 * n : 24 * n + half + 4]
+            first_ref[f, half * n : half * (n + 1)] = ref[f, 0:half]
+            second_ref[f, half * n : half * (n + 1)] = ref[f, half : 2 * half] + extra[:half]
+            rows.append((ref[f, 0:half], ref[f, 2 * half : 2 * half + 4] + extra[half:]))
+        for part in range(2):
+            sides = []
+            for side, x in ((0, 0), (1, lines - 1)):
+                start = 2 * x if part == 0 else 2 * side
+                sides.append(jnp.concatenate([r[part][start : start + 2] for r in rows], axis=0))
+            place = 4 * (fields * part + f)
+            near_out_ref[place : place + 4] = jnp.where(odd_x, sides[0], sides[1])
+            far_out_ref[place : place + 4] = jnp.where(odd_x, sides[1], sides[0])
 
 
 def prepare_kernel(alpha_ref, outer_ref, near_x_ref, far_x_ref, cells_ref, rows_ref):
@@ -290,30 +350,26 @@
             rows_ref[f, side] = left_side(passed + jnp.where(own, border, 0.0))
 
 
-def gather_kernel(near1_ref, far1_ref, near2_ref, far2_ref, near_ref, far_ref):
-    fields, lines = near1_ref.shape[0], near1_ref.shape[1] // 2
-    odd_z, odd_x = is_odd("gz"), is_odd("brick")
-    for half, near, far in ((0, near1_ref, far1_ref), (1, near2_ref, far2_ref)):
-        for f in range(fields):
-            rows = []
-            for side, x in ((0, 0), (1, lines - 1)):
-                place = 2 * x if half == 0 else 2 * lines + 2 * side
-                one, two = near[f, place : place + 2], far[f, place : place + 2]
-                rows.append(jnp.concatenate([jnp.where(odd_z, one, two), jnp.where(odd_z, two, one)], axis=0))
-            at_row = 4 * (fields * half + f)
-            near_ref[at_row : at_row + 4] = jnp.where(odd_x, rows[0], rows[1])
-            far_ref[at_row : at_row + 4] = jnp.where(odd_x, rows[1], rows[0])
-
-
-def border_kernel(alpha_ref, part_ref, near_ref, far_ref, out_ref, edge_ref, stage, sem):
+def border_kernel(alpha_ref, outer_ref, part_ref, first_ref, second_ref, out_ref, edge_ref, stage, sem):
     fields, lines, cells = part_ref.shape[:3]
+    parts = local_parts(cells)
 
     def copies(f):
         return [pltpu.make_async_copy(stage.at[f, x], out_ref.at[f, x], sem.at[f, x]) for x in range(lines)]
 
     @pl.loop(0, fields)
     def _(f):
-        border = border_term(lines, cells, alpha_column(alpha_ref[pl.ds(f, 1)]), f, near_ref, far_ref)
+        alphas = alpha_column(alpha_ref[pl.ds(f, 1)])
+        coefs = coefs_of(alphas)
+        border, line, _ = border_lanes(lines, cells, alphas)
+        direct = rows_left(border).astype(F32)
+        left = []
+        for x in range(lines):
+            local = left_side(local_matrix(parts, at(coefs, x)) * doubled(outer_ref[x : x + 1]))
+            passed = rows_left(dot(local, right_side(border * spread(line, x))))
+            left.append(jnp.concatenate([passed, jnp.where(line == x, direct, 0.0).astype(BF)], axis=1))
+        right = jnp.concatenate([four_pieces(first_ref[f]), four_pieces(second_ref[f])], axis=0)
+        border = dot(jnp.concatenate(left, axis=0), right)
         for x in range(lines):
             value = part_ref[f, x] + border[cells * x : cells * (x + 1)]
             stage[f, x] = value
@@ -335,7 +391,7 @@
 
 
 def late_kernel(
-    cells_ref, rows_ref, edge_ref, near1_ref, far1_ref, near2_ref, far2_ref, near_rows_ref, far_rows_ref, _,
+    cells_ref, rows_ref, edge_ref, near0_ref, far0_ref, near1_ref, far1_ref, near_rows_ref, far_rows_ref, _,
     out_ref, state_scr, term_scr, stage, sem,
 ):
     fields, cells, lines = edge_ref.shape[0], edge_ref.shape[2], out_ref.shape[1]
@@ -346,7 +402,10 @@
         left = jnp.concatenate([rows_ref[f, side] for f in range(fields)], axis=0)
         term_scr[side] = dot(left, right_side(state_scr[...]))
     for f in range(fields):
-        pieces = by_side(near1_ref, far1_ref, f) if f < CUT else by_side(near2_ref, far2_ref, f - CUT)
+        if f == 0:
+            pieces = by_side(near0_ref, far0_ref, slice(0, cells))
+        else:
+            pieces = by_side(near1_ref, far1_ref, f - 1)
         for side, halo in enumerate(pieces):
             term = edge_ref[f, side] + term_scr[side, cells * f : cells * (f + 1)]
             stage[f, side] = term + dot(cells_ref[f, side], right_side(halo))
@@ -394,53 +453,63 @@
 
     whole = jax.ShapeDtypeStruct(grad_field.shape, F32)
 
-    rows = shape(fields, 2 * lines, width)
-    edge, tail = shape(CUT, cells, width), shape(fields - CUT, cells, width)
-    facts, edges = shape(8, 256), shape(fields, 2, cells, width)
+    states = shape(fields, 4 * lines, width)
+    head, edge = shape(cells + 8, width), shape(fields - 1, cells, width)
+    edges = shape(fields, 2, cells, width)
+    whole_here = shape(*grad_field.shape)
     inputs = (alpha_coef, metric_inner, metric_outer, grad_field)
-    held = [pltpu.SemaphoreType.DMA((3,)), pltpu.SemaphoreType.DMA((fields, lines))]
-    near, far, edge_near, edge_far, facts_near, facts_far, alpha, inner, outer, tail_near, tail_far, field = call(
+    near, far, alpha, inner, outer = call(
+        pack_kernel,
+        GRANT,
+        [HBM] * 4,
+        [head, head, *(shape(*a.shape) for a in inputs[:3])],
+        scratch_shapes=[pltpu.SemaphoreType.DMA((5,))],
+    )(*inputs)
+    near0, far0 = swap("brick", near, far)
+    part, own, following, first, line_near, line_far = call(
         open_kernel,
         GRANT,
-        [HBM] * 4,
-        [rows, rows, edge, edge, facts, facts, *(shape(*a.shape) for a in inputs[:3]), tail, tail, shape(*grad_field.shape)],
-        scratch_shapes=held,
-    )(*inputs)
-    near_one, far_one = swap("gz", near, far)
-    near1, far1 = swap("brick", edge_near, edge_far)
-    near0, far0 = swap("brick", facts_near, facts_far)
-
-    part, near, far, first = call(
-        middle_kernel,
+        [WHOLE, WHOLE, WHOLE, HBM],
+        [whole_here, states, states, edges, edge, edge],
+        scratch_shapes=[
+            pltpu.VMEM(grad_field.shape, F32),
+            pltpu.VMEM((lines, cells, width), F32),
+            pltpu.VMEM((lines, cells, 2 * cells), F32),
+            pltpu.SemaphoreType.DMA((fields, lines)),
+        ],
+    )(alpha, inner, outer, grad_field)
+    message = shape(fields, 4 * lines + 6, width)
+    near, far = call(
+        corner_kernel,
         8,
         [WHOLE] * 6,
-        [shape(*grad_field.shape), rows, rows, edges],
-        scratch_shapes=[
-            pltpu.VMEM((lines * cells, width), F32),
-            pltpu.VMEM((lines, cells, width), F32),
-            pltpu.VMEM((lines, cells, 2 * cells), F32),
-        ],
-    )(alpha, inner, outer, field, near_one, far_one)
-    rows = shape(fields, 2 * lines + 4, width)
-    near, far = call(corner_kernel, 4, [WHOLE] * 5, [rows, rows])(near0, far0, first, near, far)
+        [message, message],
+        scratch_shapes=[pltpu.VMEM((fields, 4 * lines + 6, width), F32)] * 2,
+    )(near0, far0, outer, first, own, following)
     near_two, far_two = swap("gz", near, far)
-    near2, far2 = swap("brick", tail_near, tail_far)
+    near1, far1 = swap("brick", line_near, line_far)
 
     matrices = shape(fields, 2, cells, 3 * cells, kind=BF)
     cell_matrix, row_matrix = call(prepare_kernel, 4, [WHOLE] * 4, [matrices, matrices])(alpha, outer, near0, far0)
 
     rows = shape(8 * fields, width)
-    near, far = call(gather_kernel, 2, [WHOLE] * 4, [rows, rows])(near_one, far_one, near_two, far_two)
+    first, second, near, far = call(
+        join_kernel,
+        8,
+        [WHOLE] * 6,
+        [states, states, rows, rows],
+        scratch_shapes=[pltpu.VMEM((fields, 4 * lines + 6, width), F32)] * 2,
+    )(alpha, near0, far0, own, near_two, far_two)
     near3, far3 = swap("brick", near, far)
 
     out, edge = call(
         border_kernel,
         16,
-        [WHOLE] * 4,
+        [WHOLE] * 5,
         [whole, edges],
         outs=[HBM, WHOLE],
         scratch_shapes=[pltpu.VMEM(grad_field.shape, F32), pltpu.SemaphoreType.DMA((fields, lines))],
-    )(alpha, part, near_two, far_two)
+    )(alpha, outer, part, first, second)
 
     return call(
         late_kernel,
@@ -455,7 +524,7 @@
             pltpu.VMEM((fields, 2, cells, width), F32),
             pltpu.SemaphoreType.DMA((fields, 2)),
         ],
-    )(cell_matrix, row_matrix, edge, near1, far1, near2, far2, near3, far3, out)
+    )(cell_matrix, row_matrix, edge, near0, far0, near1, far1, near3, far3, out)
 
 
 def solution(mesh):

time: 70.8 us -> 66.1 us (0.934)
  starting transfers between devices: 25.5 us -> 17.8 us
  local copies, waits for them, and re-layouts: 0 us -> 1.19 us
  waiting for transfers between devices: 26.4 us -> 27.5 us
  Pallas kernels: 17.4 us -> 18.4 us
    ppermute x12 -> x8, starting transfers between devices: 25.5 us -> 17.8 us  [swap(): moved[kind] = lax.ppermute(value, axis, both)]
    unnamed x0 -> x10, local copies, waits for them, and re-layouts: none -> 1.19 us
    ppermute x12 -> x8, waiting for transfers between devices: 26.4 us -> 27.5 us  [swap(): moved[kind] = lax.ppermute(value, axis, both)]
    pallas_call x7, Pallas kernels: 17.4 us -> 18.4 us  [run(): pl.pallas_call(kernel, in_specs=ins, out_specs=outs if isinstance(outs, l...]
  transfers between devices with their start and end apart: 12 -> 8, of which waited for: 2 -> 1; matrix products, arithmetic and copies ran while one was open for 0% -> 0% of each run, Pallas kernels for 15% -> 24%
where the time goes in v1:
time: 66.1 us; the launch traced here: 65.1 us
  waiting for transfers between devices  27.5 us (42%)
  Pallas kernels  18.4 us (28%)
  starting transfers between devices  17.8 us (27%)
  local copies, waits for them, and re-layouts  1.19 us (2%)
    ppermute x8, waiting for transfers between devices, swap(): moved[kind] = lax.ppermute(value, axis, both)  27.5 us
    pallas_call x7, Pallas kernels, run(): pl.pallas_call(kernel, in_specs=ins, out_specs=outs if isinstance(outs, l...  18.4 us
    ppermute x8, starting transfers between devices, swap(): moved[kind] = lax.ppermute(value, axis, both)  17.8 us
  transfers between devices with their start and end apart: 8, of which 1 were waited for; matrix products, arithmetic and copies ran while one was open for 0% of the time, Pallas kernels for 24%

profile of v1, /device:TPU:41, one launch (start us, length us, event | category | flops | bytes accessed | tf_op | source)
XLA Modules:
  0.0 65.1 jit_solution(17283881142634082619)
XLA Ops:
  0.0 1.1 %shard_map.46 = (f32[72,512]{1,0:T(8,128)S(1)}, f32[72,512]{1,0:T(8,128)S(1)}, f32[5,8]{1,0:T(8,128)S(1)}, f32[8,64]{1,0:T(8,128)S(1)}, f32[8,64]{1,0:T(8,128)S(1)}) custom-call(f32[5,8]{1,0:T(8,128)} %alpha_in.1, f32[8,64]{1,0:T(8,128)} %inner_in.1, f32[8,64]{1,0:T(8,128)} %outer_in.1, f32[5,8,64,512]{3,2,1,0:T(8,128)} %field_in.3), custom_call_target="tpu_custom_call" | custom-call | tf_op jit(solution)/shard_map/pallas_call | solution.py:425
  1.1 0.0 copy-start.2
  1.1 0.6 copy-done.2
  1.7 0.0 copy-start.4
  1.7 0.6 copy-done.4
  2.3 0.0 copy-start
  2.3 0.0 copy-start.3
  2.3 0.0 collective-permute-start
  2.3 4.4 %collective-permute-start.1 = (f32[72,512]{1,0:T(8,128)S(1)}, f32[72,512]{1,0:T(8,128)S(1)}, u32[]{:S(2)}, u32[]{:S(2)}) collective-permute-start(f32[72,512]{1,0:T(8,128)S(1)} %get-tuple-element.29), channel_id=1, source_target_pairs={{16,32},{32,16},{48,64},{64,48},{80,96},{96,80},{17,33},{33,17},{4... | collective-permute-start | bytes 442376 | tf_op jit(solution)/shard_map/ppermute | solution.py:444
  6.7 0.0 copy-done
  6.7 0.0 copy-start.1
  6.7 7.5 %shard_map.48 = (f32[5,8,64,512]{3,2,1,0:T(8,128)S(1)}, f32[5,32,512]{2,1,0:T(8,128)S(1)}, f32[5,32,512]{2,1,0:T(8,128)S(1)}, f32[5,2,64,512]{3,2,1,0:T(8,128)S(...) custom-call(f32[5,8]{1,0:T(8,128)} %copy-done, f32[8,64]{1,0:T(8,128)} %copy-done.4, f32[8,64]{1,0:T(8,128)} %copy-done.2, ...), custom_call_target="tpu_custom_call" | custom-call | tf_op jit(solution)/shard_map/pallas_call | solution.py:425
  14.2 0.1 collective-permute-start.4
  14.3 4.1 %collective-permute-start.5 = (f32[4,64,512]{2,1,0:T(8,128)S(1)}, f32[4,64,512]{2,1,0:T(8,128)S(1)}, u32[]{:S(2)}, u32[]{:S(2)}) collective-permute-start(f32[4,64,512]{2,1,0:T(8,128)S(1)} %get-tuple-element.43), channel_id=1, source_target_pairs={{16,32},{32,16},{48,64},{64,48},{80,96},{96,80},{17,33},{33,17},{4... | collective-permute-start | bytes 1572872 | tf_op jit(solution)/shard_map/ppermute | solution.py:444
  18.4 0.0 collective-permute-done.near_x_ref.near0_ref
  18.4 0.0 collective-permute-done.1.far_x_ref.far0_ref
  18.4 0.0 copy-done.3
  18.4 0.6 shard_map.49
  19.0 1.9 %collective-permute-start.2 = (f32[5,38,512]{2,1,0:T(8,128)S(1)}, f32[5,38,512]{2,1,0:T(8,128)S(1)}, u32[]{:S(2)}, u32[]{:S(2)}) collective-permute-start(f32[5,38,512]{2,1,0:T(8,128)S(1)} %get-tuple-element.37), channel_id=1, source_target_pairs={{0,1},{1,0},{2,3},{3,2},{4,5},{5,4},{6,7},{7,6},{8,9},{9,8},{10,11... | collective-permute-start | bytes 1167368 | tf_op jit(solution)/shard_map/ppermute | solution.py:444
  20.8 2.7 %collective-permute-start.3 = (f32[5,38,512]{2,1,0:T(8,128)S(1)}, f32[5,38,512]{2,1,0:T(8,128)S(1)}, u32[]{:S(2)}, u32[]{:S(2)}) collective-permute-start(f32[5,38,512]{2,1,0:T(8,128)S(1)} %get-tuple-element.38), channel_id=1, source_target_pairs={{1,2},{2,1},{3,4},{4,3},{5,6},{6,5},{7,8},{8,7},{9,10},{10,9},{11,... | collective-permute-start | bytes 1167368 | tf_op jit(solution)/shard_map/ppermute | solution.py:444
  23.5 0.0 collective-permute-done.2.near_ref
  23.5 27.4 %collective-permute-done.3.far_ref = f32[5,38,512]{2,1,0:T(8,128)S(1)} collective-permute-done((f32[5,38,512]{2,1,0:T(8,128)S(1)}, f32[5,38,512]{2,1,0:T(8,128)S(1)}, u32[]{:S(2)}, u32[]{:S(2)}) %collective-permute-start.3) | collective-permute-done | bytes 389152 | tf_op jit(solution)/shard_map/ppermute | solution.py:444
  50.9 0.0 copy-done.1
  50.9 1.7 %shard_map.50 = (f32[5,32,512]{2,1,0:T(8,128)S(1)}, f32[5,32,512]{2,1,0:T(8,128)S(1)}, f32[40,512]{1,0:T(8,128)S(1)}, f32[40,512]{1,0:T(8,128)S(1)}) custom-call(f32[5,8]{1,0:T(8,128)S(1)} %copy-done.1, f32[72,512]{1,0:T(8,128)S(1)} %collective-permute-done.near_x_ref.near0_ref, f32[72,512]{1,0:T(8,128)S(1)} %collective-permute-done.1.far_x_ref.far0_ref, ...), custom_call_target="tpu_custom_call" | custom-call | tf_op jit(solution)/shard_map/pallas_call | solution.py:425
  52.6 2.1 %collective-permute-start.6 = (f32[40,512]{1,0:T(8,128)S(1)}, f32[40,512]{1,0:T(8,128)S(1)}, u32[]{:S(2)}, u32[]{:S(2)}) collective-permute-start(f32[40,512]{1,0:T(8,128)S(1)} %get-tuple-element.44), channel_id=1, source_target_pairs={{0,16},{16,0},{32,48},{48,32},{64,80},{80,64},{96,112},{112,96},{1... | collective-permute-start | bytes 245768 | tf_op jit(solution)/shard_map/ppermute | solution.py:444
  54.8 2.6 %collective-permute-start.7 = (f32[40,512]{1,0:T(8,128)S(1)}, f32[40,512]{1,0:T(8,128)S(1)}, u32[]{:S(2)}, u32[]{:S(2)}) collective-permute-start(f32[40,512]{1,0:T(8,128)S(1)} %get-tuple-element.45), channel_id=1, source_target_pairs={{16,32},{32,16},{48,64},{64,48},{80,96},{96,80},{17,33},{33,17},{4... | collective-permute-start | bytes 245768 | tf_op jit(solution)/shard_map/ppermute | solution.py:444
  57.4 1.7 %shard_map.47 = (bf16[5,2,64,192]{3,2,1,0:T(8,128)(2,1)S(1)}, bf16[5,2,64,192]{3,2,1,0:T(8,128)(2,1)S(1)}) custom-call(f32[5,8]{1,0:T(8,128)S(1)} %copy-done.1, f32[8,64]{1,0:T(8,128)S(1)} %copy-done.3, f32[72,512]{1,0:T(8,128)S(1)} %collective-permute-done.near_x_ref.near0_ref, f32[72,512]{1,0:T(8,128)S(1)} %collective-permute-done.1.far_x_ref.far0_ref), custom_call_target="tpu_custom_call" | custom-call | tf_op jit(solution)/shard_map/pallas_call | solution.py:425
  59.2 4.3 %shard_map.51 = (f32[5,8,64,512]{3,2,1,0:T(8,128)}, f32[5,2,64,512]{3,2,1,0:T(8,128)S(1)}) custom-call(f32[5,8]{1,0:T(8,128)S(1)} %copy-done.1, f32[8,64]{1,0:T(8,128)S(1)} %copy-done.3, f32[5,8,64,512]{3,2,1,0:T(8,128)S(1)} %get-tuple-element.33.part_ref, f32[5,32,512]{2,1,0:T(8,128)S(1)} %get-tuple-element.39.first_ref, ...), custom_call_target="tpu_custom_call" | custom-call | tf_op jit(solution)/shard_map/pallas_call | solution.py:425
  63.5 0.0 collective-permute-done.4.near1_ref
  63.5 0.0 collective-permute-done.5.far1_ref
  63.5 0.0 collective-permute-done.6.near_rows_ref
  63.5 0.0 collective-permute-done.7.far_rows_ref
  63.5 1.5 %shard_map.52 = f32[5,8,64,512]{3,2,1,0:T(8,128)} custom-call(bf16[5,2,64,192]{3,2,1,0:T(8,128)(2,1)S(1)} %get-tuple-element.30.cells_ref, bf16[5,2,64,192]{3,2,1,0:T(8,128)(2,1)S(1)} %get-tuple-element.31.rows_ref, f32[5,2,64,512]{3,2,1,0:T(8,128)S(1)} %get-tuple-element.41.edge_ref, ...), custom_call_target="tpu_custom_call", output_to_operand_aliasing={{}: (9, {})} | custom-call | tf_op jit(solution)/shard_map/pallas_call | solution.py:425
Async XLA Ops:
  1.1 0.6 copy-start.2
  1.7 0.6 copy-start.4
  2.3 4.4 %copy-start = (f32[5,8]{1,0:T(8,128)}, f32[5,8]{1,0:T(8,128)S(1)}, u32[]{:S(2)}) copy-start(f32[5,8]{1,0:T(8,128)S(1)} %get-tuple-element.26.alpha_ref) | copy-start | bytes 484
  2.3 16.1 %copy-start.3 = (f32[8,64]{1,0:T(8,128)S(1)}, f32[8,64]{1,0:T(8,128)}, u32[]{:S(2)}) copy-start(f32[8,64]{1,0:T(8,128)} %copy-done.2) | copy-start | bytes 6148
  2.3 16.0 %collective-permute-start = (f32[72,512]{1,0:T(8,128)S(1)}, f32[72,512]{1,0:T(8,128)S(1)}, u32[]{:S(2)}, u32[]{:S(2)}) collective-permute-start(f32[72,512]{1,0:T(8,128)S(1)} %get-tuple-element.28), channel_id=1, source_target_pairs={{0,16},{16,0},{32,48},{48,32},{64,80},{80,64},{96,112},{112,96},{1... | collective-permute-start | bytes 442376 | tf_op jit(solution)/shard_map/ppermute | solution.py:444
  2.3 16.1 %collective-permute-start.1 = (f32[72,512]{1,0:T(8,128)S(1)}, f32[72,512]{1,0:T(8,128)S(1)}, u32[]{:S(2)}, u32[]{:S(2)}) collective-permute-start(f32[72,512]{1,0:T(8,128)S(1)} %get-tuple-element.29), channel_id=1, source_target_pairs={{16,32},{32,16},{48,64},{64,48},{80,96},{96,80},{17,33},{33,17},{4... | collective-permute-start | bytes 442376 | tf_op jit(solution)/shard_map/ppermute | solution.py:444
  6.7 44.2 %copy-start.1 = (f32[5,8]{1,0:T(8,128)S(1)}, f32[5,8]{1,0:T(8,128)}, u32[]{:S(2)}) copy-start(f32[5,8]{1,0:T(8,128)} %copy-done) | copy-start | bytes 484
  14.2 49.3 %collective-permute-start.4 = (f32[4,64,512]{2,1,0:T(8,128)S(1)}, f32[4,64,512]{2,1,0:T(8,128)S(1)}, u32[]{:S(2)}, u32[]{:S(2)}) collective-permute-start(f32[4,64,512]{2,1,0:T(8,128)S(1)} %get-tuple-element.42), channel_id=1, source_target_pairs={{0,16},{16,0},{32,48},{48,32},{64,80},{80,64},{96,112},{112,96},{1... | collective-permute-start | bytes 1572872 | tf_op jit(solution)/shard_map/ppermute | solution.py:444
  14.3 49.2 %collective-permute-start.5 = (f32[4,64,512]{2,1,0:T(8,128)S(1)}, f32[4,64,512]{2,1,0:T(8,128)S(1)}, u32[]{:S(2)}, u32[]{:S(2)}) collective-permute-start(f32[4,64,512]{2,1,0:T(8,128)S(1)} %get-tuple-element.43), channel_id=1, source_target_pairs={{16,32},{32,16},{48,64},{64,48},{80,96},{96,80},{17,33},{33,17},{4... | collective-permute-start | bytes 1572872 | tf_op jit(solution)/shard_map/ppermute | solution.py:444
  19.0 4.5 %collective-permute-start.2 = (f32[5,38,512]{2,1,0:T(8,128)S(1)}, f32[5,38,512]{2,1,0:T(8,128)S(1)}, u32[]{:S(2)}, u32[]{:S(2)}) collective-permute-start(f32[5,38,512]{2,1,0:T(8,128)S(1)} %get-tuple-element.37), channel_id=1, source_target_pairs={{0,1},{1,0},{2,3},{3,2},{4,5},{5,4},{6,7},{7,6},{8,9},{9,8},{10,11... | collective-permute-start | bytes 1167368 | tf_op jit(solution)/shard_map/ppermute | solution.py:444
  20.8 30.1 %collective-permute-start.3 = (f32[5,38,512]{2,1,0:T(8,128)S(1)}, f32[5,38,512]{2,1,0:T(8,128)S(1)}, u32[]{:S(2)}, u32[]{:S(2)}) collective-permute-start(f32[5,38,512]{2,1,0:T(8,128)S(1)} %get-tuple-element.38), channel_id=1, source_target_pairs={{1,2},{2,1},{3,4},{4,3},{5,6},{6,5},{7,8},{8,7},{9,10},{10,9},{11,... | collective-permute-start | bytes 1167368 | tf_op jit(solution)/shard_map/ppermute | solution.py:444
  52.6 10.9 %collective-permute-start.6 = (f32[40,512]{1,0:T(8,128)S(1)}, f32[40,512]{1,0:T(8,128)S(1)}, u32[]{:S(2)}, u32[]{:S(2)}) collective-permute-start(f32[40,512]{1,0:T(8,128)S(1)} %get-tuple-element.44), channel_id=1, source_target_pairs={{0,16},{16,0},{32,48},{48,32},{64,80},{80,64},{96,112},{112,96},{1... | collective-permute-start | bytes 245768 | tf_op jit(solution)/shard_map/ppermute | solution.py:444
  54.8 8.7 %collective-permute-start.7 = (f32[40,512]{1,0:T(8,128)S(1)}, f32[40,512]{1,0:T(8,128)S(1)}, u32[]{:S(2)}, u32[]{:S(2)}) collective-permute-start(f32[40,512]{1,0:T(8,128)S(1)} %get-tuple-element.45), channel_id=1, source_target_pairs={{16,32},{32,16},{48,64},{64,48},{80,96},{96,80},{17,33},{33,17},{4... | collective-permute-start | bytes 245768 | tf_op jit(solution)/shard_map/ppermute | solution.py:444

commit v2 on v1

--- a/solution.py
+++ b/solution.py
@@ -9,6 +9,7 @@
 BF = jnp.bfloat16
 F32 = jnp.float32
 GRANT = 54
+CUT = 2
 AHEAD = 3
 
 
@@ -183,7 +184,7 @@
 
 def open_kernel(
     alpha_ref, inner_ref, outer_ref, field_in,
-    part_ref, own_ref, next_ref, edge_ref, line_near_ref, line_far_ref, field_ref, first_scr, local_scr, field_sem,
+    part_ref, own_ref, next_ref, edge_ref, line_near_ref, line_far_ref, tail_near_ref, tail_far_ref, field_ref, first_scr, local_scr, field_sem,
 ):
     fields, lines, cells = field_ref.shape[:3]
     odd = is_odd("brick")
@@ -222,9 +223,10 @@
         edge_ref[f, 1] = first_scr[lines - 1]
 
     for f in range(1, fields):
+        near, far, n = (line_near_ref, line_far_ref, f - 1) if f < CUT else (tail_near_ref, tail_far_ref, f - CUT)
         low, high = field_ref[f, 0], field_ref[f, lines - 1]
-        line_near_ref[f - 1] = jnp.where(odd, low, high)
-        line_far_ref[f - 1] = jnp.where(odd, high, low)
+        near[n] = jnp.where(odd, low, high)
+        far[n] = jnp.where(odd, high, low)
 
 
 def corner_kernel(
@@ -391,7 +393,7 @@
 
 
 def late_kernel(
-    cells_ref, rows_ref, edge_ref, near0_ref, far0_ref, near1_ref, far1_ref, near_rows_ref, far_rows_ref, _,
+    cells_ref, rows_ref, edge_ref, near0_ref, far0_ref, near1_ref, far1_ref, near2_ref, far2_ref, near_rows_ref, far_rows_ref, _,
     out_ref, state_scr, term_scr, stage, sem,
 ):
     fields, cells, lines = edge_ref.shape[0], edge_ref.shape[2], out_ref.shape[1]
@@ -405,7 +407,7 @@
         if f == 0:
             pieces = by_side(near0_ref, far0_ref, slice(0, cells))
         else:
-            pieces = by_side(near1_ref, far1_ref, f - 1)
+            pieces = by_side(near1_ref, far1_ref, f - 1) if f < CUT else by_side(near2_ref, far2_ref, f - CUT)
         for side, halo in enumerate(pieces):
             term = edge_ref[f, side] + term_scr[side, cells * f : cells * (f + 1)]
             stage[f, side] = term + dot(cells_ref[f, side], right_side(halo))
@@ -454,11 +456,11 @@
     whole = jax.ShapeDtypeStruct(grad_field.shape, F32)
 
     states = shape(fields, 4 * lines, width)
-    head, edge = shape(cells + 8, width), shape(fields - 1, cells, width)
+    head, edge, tail = shape(cells + 8, width), shape(CUT - 1, cells, width), shape(fields - CUT, cells, width)
     edges = shape(fields, 2, cells, width)
     whole_here = shape(*grad_field.shape)
     inputs = (alpha_coef, metric_inner, metric_outer, grad_field)
-    near, far, alpha, inner, outer = call(
+    near, far, _, _, _ = call(
         pack_kernel,
         GRANT,
         [HBM] * 4,
@@ -466,18 +468,18 @@
         scratch_shapes=[pltpu.SemaphoreType.DMA((5,))],
     )(*inputs)
     near0, far0 = swap("brick", near, far)
-    part, own, following, first, line_near, line_far = call(
+    part, own, following, first, line_near, line_far, tail_near, tail_far = call(
         open_kernel,
-        GRANT,
+        GRANT - 2,
         [WHOLE, WHOLE, WHOLE, HBM],
-        [whole_here, states, states, edges, edge, edge],
+        [whole_here, states, states, edges, edge, edge, tail, tail],
         scratch_shapes=[
             pltpu.VMEM(grad_field.shape, F32),
             pltpu.VMEM((lines, cells, width), F32),
             pltpu.VMEM((lines, cells, 2 * cells), F32),
             pltpu.SemaphoreType.DMA((fields, lines)),
         ],
-    )(alpha, inner, outer, grad_field)
+    )(alpha_coef, metric_inner, metric_outer, grad_field)
     message = shape(fields, 4 * lines + 6, width)
     near, far = call(
         corner_kernel,
@@ -485,12 +487,13 @@
         [WHOLE] * 6,
         [message, message],
         scratch_shapes=[pltpu.VMEM((fields, 4 * lines + 6, width), F32)] * 2,
-    )(near0, far0, outer, first, own, following)
+    )(near0, far0, metric_outer, first, own, following)
     near_two, far_two = swap("gz", near, far)
     near1, far1 = swap("brick", line_near, line_far)
+    near2, far2 = swap("brick", tail_near, tail_far)
 
     matrices = shape(fields, 2, cells, 3 * cells, kind=BF)
-    cell_matrix, row_matrix = call(prepare_kernel, 4, [WHOLE] * 4, [matrices, matrices])(alpha, outer, near0, far0)
+    cell_matrix, row_matrix = call(prepare_kernel, 4, [WHOLE] * 4, [matrices, matrices])(alpha_coef, metric_outer, near0, far0)
 
     rows = shape(8 * fields, width)
     first, second, near, far = call(
@@ -499,7 +502,7 @@
         [WHOLE] * 6,
         [states, states, rows, rows],
         scratch_shapes=[pltpu.VMEM((fields, 4 * lines + 6, width), F32)] * 2,
-    )(alpha, near0, far0, own, near_two, far_two)
+    )(alpha_coef, near0, far0, own, near_two, far_two)
     near3, far3 = swap("brick", near, far)
 
     out, edge = call(
@@ -509,22 +512,22 @@
         [whole, edges],
         outs=[HBM, WHOLE],
         scratch_shapes=[pltpu.VMEM(grad_field.shape, F32), pltpu.SemaphoreType.DMA((fields, lines))],
-    )(alpha, outer, part, first, second)
+    )(alpha_coef, metric_outer, part, first, second)
 
     return call(
         late_kernel,
         8,
-        [WHOLE] * 9 + [HBM],
+        [WHOLE] * 11 + [HBM],
         whole,
         outs=HBM,
-        input_output_aliases={9: 0},
+        input_output_aliases={11: 0},
         scratch_shapes=[
             pltpu.VMEM((cells, width), F32),
             pltpu.VMEM((2, fields * cells, width), F32),
             pltpu.VMEM((fields, 2, cells, width), F32),
             pltpu.SemaphoreType.DMA((fields, 2)),
         ],
-    )(cell_matrix, row_matrix, edge, near0, far0, near1, far1, near3, far3, out)
+    )(cell_matrix, row_matrix, edge, near0, far0, near1, far1, near2, far2, near3, far3, out)
 
 
 def solution(mesh):

time: 66.1 us -> 63.5 us (0.961)
  waiting for transfers between devices: 27.5 us -> 23.9 us
  starting transfers between devices: 17.8 us -> 19.9 us
  local copies, waits for them, and re-layouts: 1.19 us -> 0.01 us
    ppermute x8 -> x10, waiting for transfers between devices: 27.5 us -> 23.9 us  [swap(): moved[kind] = lax.ppermute(value, axis, both)]
    ppermute x8 -> x10, starting transfers between devices: 17.8 us -> 19.9 us  [swap(): moved[kind] = lax.ppermute(value, axis, both)]
    unnamed x10 -> x4, local copies, waits for them, and re-layouts: 1.19 us -> 0.01 us
  transfers between devices with their start and end apart: 8 -> 10, of which waited for: 1 -> 2; matrix products, arithmetic and copies ran while one was open for 0% -> 0% of each run, Pallas kernels for 24% -> 24%
where the time goes in v2:
time: 63.5 us; the launch traced here: 63 us
  waiting for transfers between devices  23.9 us (38%)
  starting transfers between devices  19.9 us (31%)
  Pallas kernels  18.9 us (30%)
    ppermute x10, waiting for transfers between devices, swap(): moved[kind] = lax.ppermute(value, axis, both)  23.9 us
    ppermute x10, starting transfers between devices, swap(): moved[kind] = lax.ppermute(value, axis, both)  19.9 us
    pallas_call x7, Pallas kernels, run(): pl.pallas_call(kernel, in_specs=ins, out_specs=outs if isinstance(outs, l...  18.9 us
  transfers between devices with their start and end apart: 10, of which 2 were waited for; matrix products, arithmetic and copies ran while one was open for 0% of the time, Pallas kernels for 24%

profile of v2, /device:TPU:41, one launch (start us, length us, event | category | flops | bytes accessed | tf_op | source)
XLA Modules:
  0.0 63.0 jit_solution(13074750632986040956)
XLA Ops:
  0.0 0.0 copy-start
  0.0 0.0 copy-start.1
  0.0 1.7 %shard_map.46 = (f32[72,512]{1,0:T(8,128)S(1)}, f32[72,512]{1,0:T(8,128)S(1)}, f32[5,8]{1,0:T(8,128)}, f32[8,64]{1,0:T(8,128)}, f32[8,64]{1,0:T(8,128)}) custom-call(f32[5,8]{1,0:T(8,128)} %alpha_ref.7, f32[8,64]{1,0:T(8,128)} %inner_ref.1, f32[8,64]{1,0:T(8,128)} %outer_ref.7, f32[5,8,64,512]{3,2,1,0:T(8,128)} %field_in.3), custom_call_target="tpu_custom_call" | custom-call | tf_op jit(solution)/shard_map/pallas_call | solution.py:427
  1.7 0.1 collective-permute-start
  1.8 4.4 %collective-permute-start.1 = (f32[72,512]{1,0:T(8,128)S(1)}, f32[72,512]{1,0:T(8,128)S(1)}, u32[]{:S(2)}, u32[]{:S(2)}) collective-permute-start(f32[72,512]{1,0:T(8,128)S(1)} %get-tuple-element.26), channel_id=1, source_target_pairs={{16,32},{32,16},{48,64},{64,48},{80,96},{96,80},{17,33},{33,17},{4... | collective-permute-start | bytes 442376 | tf_op jit(solution)/shard_map/ppermute | solution.py:446
  6.2 7.4 %shard_map.48 = (f32[5,8,64,512]{3,2,1,0:T(8,128)S(1)}, f32[5,32,512]{2,1,0:T(8,128)S(1)}, f32[5,32,512]{2,1,0:T(8,128)S(1)}, f32[5,2,64,512]{3,2,1,0:T(8,128)S(...) custom-call(f32[5,8]{1,0:T(8,128)} %alpha_ref.7, ...), custom_call_target="tpu_custom_call" | custom-call | tf_op jit(solution)/shard_map/pallas_call | solution.py:427
  13.6 0.0 collective-permute-done.near_x_ref.near0_ref
  13.6 0.0 collective-permute-done.1.far_x_ref.far0_ref
  13.6 0.0 copy-done.1
  13.6 0.6 shard_map.49
  14.2 1.3 %collective-permute-start.2 = (f32[5,38,512]{2,1,0:T(8,128)S(1)}, f32[5,38,512]{2,1,0:T(8,128)S(1)}, u32[]{:S(2)}, u32[]{:S(2)}) collective-permute-start(f32[5,38,512]{2,1,0:T(8,128)S(1)} %get-tuple-element.33), channel_id=1, source_target_pairs={{0,1},{1,0},{2,3},{3,2},{4,5},{5,4},{6,7},{7,6},{8,9},{9,8},{10,11... | collective-permute-start | bytes 1167368 | tf_op jit(solution)/shard_map/ppermute | solution.py:446
  15.5 2.7 %collective-permute-start.3 = (f32[5,38,512]{2,1,0:T(8,128)S(1)}, f32[5,38,512]{2,1,0:T(8,128)S(1)}, u32[]{:S(2)}, u32[]{:S(2)}) collective-permute-start(f32[5,38,512]{2,1,0:T(8,128)S(1)} %get-tuple-element.34), channel_id=1, source_target_pairs={{1,2},{2,1},{3,4},{4,3},{5,6},{6,5},{7,8},{8,7},{9,10},{10,9},{11,... | collective-permute-start | bytes 1167368 | tf_op jit(solution)/shard_map/ppermute | solution.py:446
  18.2 0.0 collective-permute-start.6
  18.2 4.1 %collective-permute-start.7 = (f32[3,64,512]{2,1,0:T(8,128)S(1)}, f32[3,64,512]{2,1,0:T(8,128)S(1)}, u32[]{:S(2)}, u32[]{:S(2)}) collective-permute-start(f32[3,64,512]{2,1,0:T(8,128)S(1)} %get-tuple-element.41), channel_id=1, source_target_pairs={{16,32},{32,16},{48,64},{64,48},{80,96},{96,80},{17,33},{33,17},{4... | collective-permute-start | bytes 1179656 | tf_op jit(solution)/shard_map/ppermute | solution.py:446
  22.3 0.1 collective-permute-start.4
  22.3 0.0 collective-permute-done.2.near_ref
  22.4 2.8 %collective-permute-start.5 = (f32[1,64,512]{2,1,0:T(8,128)S(1)}, f32[1,64,512]{2,1,0:T(8,128)S(1)}, u32[]{:S(2)}, u32[]{:S(2)}) collective-permute-start(f32[1,64,512]{2,1,0:T(8,128)S(1)} %get-tuple-element.39), channel_id=1, source_target_pairs={{16,32},{32,16},{48,64},{64,48},{80,96},{96,80},{17,33},{33,17},{4... | collective-permute-start | bytes 393224 | tf_op jit(solution)/shard_map/ppermute | solution.py:446
  25.2 18.9 %collective-permute-done.3.far_ref = f32[5,38,512]{2,1,0:T(8,128)S(1)} collective-permute-done((f32[5,38,512]{2,1,0:T(8,128)S(1)}, f32[5,38,512]{2,1,0:T(8,128)S(1)}, u32[]{:S(2)}, u32[]{:S(2)}) %collective-permute-start.3) | collective-permute-done | bytes 389152 | tf_op jit(solution)/shard_map/ppermute | solution.py:446
  44.0 0.0 copy-done
  44.1 1.7 %shard_map.50 = (f32[5,32,512]{2,1,0:T(8,128)S(1)}, f32[5,32,512]{2,1,0:T(8,128)S(1)}, f32[40,512]{1,0:T(8,128)S(1)}, f32[40,512]{1,0:T(8,128)S(1)}) custom-call(f32[5,8]{1,0:T(8,128)S(1)} %copy-done, f32[72,512]{1,0:T(8,128)S(1)} %collective-permute-done.near_x_ref.near0_ref, f32[72,512]{1,0:T(8,128)S(1)} %collective-permute-done.1.far_x_ref.far0_ref, ...), custom_call_target="tpu_custom_call" | custom-call | tf_op jit(solution)/shard_map/pallas_call | solution.py:427
  45.8 0.1 collective-permute-start.8
  45.8 5.0 %collective-permute-done.4.near1_ref = f32[1,64,512]{2,1,0:T(8,128)S(1)} collective-permute-done((f32[1,64,512]{2,1,0:T(8,128)S(1)}, f32[1,64,512]{2,1,0:T(8,128)S(1)}, u32[]{:S(2)}, u32[]{:S(2)}) %collective-permute-start.4) | collective-permute-done | bytes 131104 | tf_op jit(solution)/shard_map/ppermute | solution.py:446
  50.8 4.5 %collective-permute-start.9 = (f32[40,512]{1,0:T(8,128)S(1)}, f32[40,512]{1,0:T(8,128)S(1)}, u32[]{:S(2)}, u32[]{:S(2)}) collective-permute-start(f32[40,512]{1,0:T(8,128)S(1)} %get-tuple-element.43), channel_id=1, source_target_pairs={{16,32},{32,16},{48,64},{64,48},{80,96},{96,80},{17,33},{33,17},{4... | collective-permute-start | bytes 245768 | tf_op jit(solution)/shard_map/ppermute | solution.py:446
  55.3 1.7 %shard_map.47 = (bf16[5,2,64,192]{3,2,1,0:T(8,128)(2,1)S(1)}, bf16[5,2,64,192]{3,2,1,0:T(8,128)(2,1)S(1)}) custom-call(f32[5,8]{1,0:T(8,128)S(1)} %copy-done, f32[8,64]{1,0:T(8,128)S(1)} %copy-done.1, f32[72,512]{1,0:T(8,128)S(1)} %collective-permute-done.near_x_ref.near0_ref, f32[72,512]{1,0:T(8,128)S(1)} %collective-permute-done.1.far_x_ref.far0_ref), custom_call_target="tpu_custom_call" | custom-call | tf_op jit(solution)/shard_map/pallas_call | solution.py:427
  57.1 4.3 %shard_map.51 = (f32[5,8,64,512]{3,2,1,0:T(8,128)}, f32[5,2,64,512]{3,2,1,0:T(8,128)S(1)}) custom-call(f32[5,8]{1,0:T(8,128)S(1)} %copy-done, f32[8,64]{1,0:T(8,128)S(1)} %copy-done.1, f32[5,8,64,512]{3,2,1,0:T(8,128)S(1)} %get-tuple-element.29.part_ref, f32[5,32,512]{2,1,0:T(8,128)S(1)} %get-tuple-element.35.first_ref, ...), custom_call_target="tpu_custom_call" | custom-call | tf_op jit(solution)/shard_map/pallas_call | solution.py:427
  61.4 0.0 collective-permute-done.5.far1_ref
  61.4 0.0 collective-permute-done.6.near2_ref
  61.4 0.0 collective-permute-done.7.far2_ref
  61.4 0.0 collective-permute-done.8.near_rows_ref
  61.4 0.0 collective-permute-done.9.far_rows_ref
  61.4 1.5 %shard_map.52 = f32[5,8,64,512]{3,2,1,0:T(8,128)} custom-call(bf16[5,2,64,192]{3,2,1,0:T(8,128)(2,1)S(1)} %get-tuple-element.27.cells_ref, bf16[5,2,64,192]{3,2,1,0:T(8,128)(2,1)S(1)} %get-tuple-element.28.rows_ref, f32[5,2,64,512]{3,2,1,0:T(8,128)S(1)} %get-tuple-element.37.edge_ref, ...), custom_call_target="tpu_custom_call", output_to_operand_aliasing={{}: (11, {})} | custom-call | tf_op jit(solution)/shard_map/pallas_call | solution.py:427
Async XLA Ops:
  0.0 44.1 %copy-start = (f32[5,8]{1,0:T(8,128)S(1)}, f32[5,8]{1,0:T(8,128)}, u32[]{:S(2)}) copy-start(f32[5,8]{1,0:T(8,128)} %alpha_ref.7) | copy-start | bytes 484
  0.0 13.6 %copy-start.1 = (f32[8,64]{1,0:T(8,128)S(1)}, f32[8,64]{1,0:T(8,128)}, u32[]{:S(2)}) copy-start(f32[8,64]{1,0:T(8,128)} %outer_ref.7) | copy-start | bytes 6148
  1.7 11.9 %collective-permute-start = (f32[72,512]{1,0:T(8,128)S(1)}, f32[72,512]{1,0:T(8,128)S(1)}, u32[]{:S(2)}, u32[]{:S(2)}) collective-permute-start(f32[72,512]{1,0:T(8,128)S(1)} %get-tuple-element.25), channel_id=1, source_target_pairs={{0,16},{16,0},{32,48},{48,32},{64,80},{80,64},{96,112},{112,96},{1... | collective-permute-start | bytes 442376 | tf_op jit(solution)/shard_map/ppermute | solution.py:446
  1.8 11.8 %collective-permute-start.1 = (f32[72,512]{1,0:T(8,128)S(1)}, f32[72,512]{1,0:T(8,128)S(1)}, u32[]{:S(2)}, u32[]{:S(2)}) collective-permute-start(f32[72,512]{1,0:T(8,128)S(1)} %get-tuple-element.26), channel_id=1, source_target_pairs={{16,32},{32,16},{48,64},{64,48},{80,96},{96,80},{17,33},{33,17},{4... | collective-permute-start | bytes 442376 | tf_op jit(solution)/shard_map/ppermute | solution.py:446
  14.2 8.2 %collective-permute-start.2 = (f32[5,38,512]{2,1,0:T(8,128)S(1)}, f32[5,38,512]{2,1,0:T(8,128)S(1)}, u32[]{:S(2)}, u32[]{:S(2)}) collective-permute-start(f32[5,38,512]{2,1,0:T(8,128)S(1)} %get-tuple-element.33), channel_id=1, source_target_pairs={{0,1},{1,0},{2,3},{3,2},{4,5},{5,4},{6,7},{7,6},{8,9},{9,8},{10,11... | collective-permute-start | bytes 1167368 | tf_op jit(solution)/shard_map/ppermute | solution.py:446
  15.5 28.6 %collective-permute-start.3 = (f32[5,38,512]{2,1,0:T(8,128)S(1)}, f32[5,38,512]{2,1,0:T(8,128)S(1)}, u32[]{:S(2)}, u32[]{:S(2)}) collective-permute-start(f32[5,38,512]{2,1,0:T(8,128)S(1)} %get-tuple-element.34), channel_id=1, source_target_pairs={{1,2},{2,1},{3,4},{4,3},{5,6},{6,5},{7,8},{8,7},{9,10},{10,9},{11,... | collective-permute-start | bytes 1167368 | tf_op jit(solution)/shard_map/ppermute | solution.py:446
  18.2 43.2 %collective-permute-start.6 = (f32[3,64,512]{2,1,0:T(8,128)S(1)}, f32[3,64,512]{2,1,0:T(8,128)S(1)}, u32[]{:S(2)}, u32[]{:S(2)}) collective-permute-start(f32[3,64,512]{2,1,0:T(8,128)S(1)} %get-tuple-element.40), channel_id=1, source_target_pairs={{0,16},{16,0},{32,48},{48,32},{64,80},{80,64},{96,112},{112,96},{1... | collective-permute-start | bytes 1179656 | tf_op jit(solution)/shard_map/ppermute | solution.py:446
  18.2 43.2 %collective-permute-start.7 = (f32[3,64,512]{2,1,0:T(8,128)S(1)}, f32[3,64,512]{2,1,0:T(8,128)S(1)}, u32[]{:S(2)}, u32[]{:S(2)}) collective-permute-start(f32[3,64,512]{2,1,0:T(8,128)S(1)} %get-tuple-element.41), channel_id=1, source_target_pairs={{16,32},{32,16},{48,64},{64,48},{80,96},{96,80},{17,33},{33,17},{4... | collective-permute-start | bytes 1179656 | tf_op jit(solution)/shard_map/ppermute | solution.py:446
  22.3 28.6 %collective-permute-start.4 = (f32[1,64,512]{2,1,0:T(8,128)S(1)}, f32[1,64,512]{2,1,0:T(8,128)S(1)}, u32[]{:S(2)}, u32[]{:S(2)}) collective-permute-start(f32[1,64,512]{2,1,0:T(8,128)S(1)} %get-tuple-element.38), channel_id=1, source_target_pairs={{0,16},{16,0},{32,48},{48,32},{64,80},{80,64},{96,112},{112,96},{1... | collective-permute-start | bytes 393224 | tf_op jit(solution)/shard_map/ppermute | solution.py:446
  22.4 39.0 %collective-permute-start.5 = (f32[1,64,512]{2,1,0:T(8,128)S(1)}, f32[1,64,512]{2,1,0:T(8,128)S(1)}, u32[]{:S(2)}, u32[]{:S(2)}) collective-permute-start(f32[1,64,512]{2,1,0:T(8,128)S(1)} %get-tuple-element.39), channel_id=1, source_target_pairs={{16,32},{32,16},{48,64},{64,48},{80,96},{96,80},{17,33},{33,17},{4... | collective-permute-start | bytes 393224 | tf_op jit(solution)/shard_map/ppermute | solution.py:446
  45.8 15.7 %collective-permute-start.8 = (f32[40,512]{1,0:T(8,128)S(1)}, f32[40,512]{1,0:T(8,128)S(1)}, u32[]{:S(2)}, u32[]{:S(2)}) collective-permute-start(f32[40,512]{1,0:T(8,128)S(1)} %get-tuple-element.42), channel_id=1, source_target_pairs={{0,16},{16,0},{32,48},{48,32},{64,80},{80,64},{96,112},{112,96},{1... | collective-permute-start | bytes 245768 | tf_op jit(solution)/shard_map/ppermute | solution.py:446
  50.8 10.6 %collective-permute-start.9 = (f32[40,512]{1,0:T(8,128)S(1)}, f32[40,512]{1,0:T(8,128)S(1)}, u32[]{:S(2)}, u32[]{:S(2)}) collective-permute-start(f32[40,512]{1,0:T(8,128)S(1)} %get-tuple-element.43), channel_id=1, source_target_pairs={{16,32},{32,16},{48,64},{64,48},{80,96},{96,80},{17,33},{33,17},{4... | collective-permute-start | bytes 245768 | tf_op jit(solution)/shard_map/ppermute | solution.py:446
